TPU v7x, 256 devices: a whole 4x4x8 slice. The times are simulated.
256 devices in a mesh: clip: 128 (over z, y, x), mp: 2 (over core).
Axes of the slice: x: 4, y: 4, z: 8, core: 2. Of those that a mesh axis runs over, the one named last changes fastest.
Arguments:
- tokens: bfloat16 [384, 128, 1024], P('clip', None, 'mp'), may hold values from -6 to 6
- bottleneck: bfloat16 [128, 4, 1024], P('clip', None, 'mp'), may hold values from -6 to 6
- clip_lengths: int32 [128], replicated, may hold values from 2 to 4, as said below
- video_blocks: int32 [128], replicated, may hold values from 1 to 3, as said below
- store_map: int32 [128, 3], replicated, may hold values from -1 to 511, as said below
- norm1_gain: float32 [1024], replicated, may hold values from 0.4 to 1.6
- w_qkv: bfloat16 [3, 1024, 1024], P(None, None, 'mp'), may hold values from -0.625 to 0.625
- w_out: bfloat16 [1024, 1024], P('mp'), may hold values from -0.1875 to 0.1875
- norm2_gain: float32 [1024], replicated, may hold values from 0.4 to 1.6
- w_up: bfloat16 [1024, 4096], P(None, 'mp'), may hold values from -0.1875 to 0.1875
- w_down: bfloat16 [4096, 1024], P('mp'), may hold values from -0.09375 to 0.09375
Outputs:
- mixed_tokens: bfloat16 [384, 128, 1024], P('clip', None, 'mp')
- merged_bottleneck: bfloat16 [128, 4, 1024], P('clip', None, 'mp')
Inputs may be any that keep to these rules, and one draw needn't show every extreme that they name: clip_lengths[c] counts the blocks of the clip owned by index c of clip. The first video_blocks[c] blocks of clip c are video, the others up to clip_lengths[c] audio; video_blocks[c] <= clip_lengths[c] - 1. store_map[d, s] = c * 4 + b when slot s of device d along clip holds block b of clip c, and -1 when the slot is empty; each block b < clip_lengths[c] of each clip sits in exactly one slot, on a device of the same aligned group of 4 devices along clip as c; no device holds two blocks of one clip.
All inputs are finite; a program needn't handle non-finite values.
Results may differ from a plain program's by a relative error of at most 0.006.
Values may be sent and summed in bfloat16 or wider, within the bound.
No kernel may reach another device: no remote copies, remote signals or barrier semaphores. Data moves between devices by JAX's collectives and lax.ppermute only.
A program may use at most 128 MiB of HBM per device.

v0:
```python
import functools

import jax
import jax.numpy as jnp
from jax import lax
from jax.experimental import pallas as pl
from jax.experimental.pallas import tpu as pltpu
from jax.sharding import PartitionSpec as P

HEAD_DIM = 64
BLK = 128
NB = 4
SLOT_DEV = 4
STORE_DEV = 3
GROUP = 4
PAD = 16
STORED = STORE_DEV * BLK
ROWS = STORED + PAD
CLIP_ROWS = SLOT_DEV * BLK
BF16 = jnp.bfloat16
F32 = jnp.float32

VMEM = pl.BlockSpec(memory_space=pltpu.VMEM)
SMEM = pl.BlockSpec(memory_space=pltpu.SMEM)


def spec(shape, dtype=BF16):
    return jax.ShapeDtypeStruct(shape, dtype)


def partner(x, step):
    return lax.ppermute(x, "clip", [(i, i ^ step) for i in range(lax.axis_size("clip"))])


def slot_for(store_map, device, owner):
    slot = jnp.int32(-1)
    block = jnp.int32(-1)
    for s in range(STORE_DEV):
        entry = store_map[device, s]
        hit = (entry >= 0) & (entry // SLOT_DEV == owner)
        slot = jnp.where(hit, s, slot)
        block = jnp.where(hit, entry % SLOT_DEV, block)
    return slot, block


def norm_into(x0, x1, gain, out, at, rows):
    half = x0.shape[1]
    x0 = x0.astype(F32)
    x1 = x1.astype(F32)
    scale = 1.0 / (2 * half)
    mean = (jnp.sum(x0, axis=-1, keepdims=True) + jnp.sum(x1, axis=-1, keepdims=True)) * scale
    x0 = x0 - mean
    x1 = x1 - mean
    moment = (
        jnp.sum(x0 * x0, axis=-1, keepdims=True) + jnp.sum(x1 * x1, axis=-1, keepdims=True)
    ) * scale
    inv = lax.rsqrt(moment + 1e-05)
    out[pl.ds(at, rows), :half] = (x0 * inv * gain[:, :half]).astype(BF16)
    out[pl.ds(at, rows), half:] = (x1 * inv * gain[:, half:]).astype(BF16)


def pack_kernel(store_map, tokens, extra, near, across, far, stored):
    member = lax.axis_index("clip")
    for step, out in ((1, near), (3, across), (2, far)):
        slot, _ = slot_for(store_map, member, member ^ step)

        @pl.when(slot >= 0)
        def _():
            out[...] = tokens[jnp.maximum(slot, 0)]

        @pl.when(slot < 0)
        def _():
            out[...] = jnp.zeros_like(out)

    for s in range(STORE_DEV):
        stored[s * BLK : (s + 1) * BLK, :] = tokens[s]
    width = stored.shape[1]
    stored[STORED:, :] = jnp.concatenate(
        [extra[0].astype(F32), jnp.zeros((PAD - NB, width), F32)], axis=0
    ).astype(BF16)


def attend_kernel(
    store_map,
    lengths,
    videos,
    stored,
    arrived,
    gain,
    w_qkv,
    near,
    across,
    far,
    own,
    normed,
    query,
    keys,
    values,
    context,
):
    member = lax.axis_index("clip")
    length = lengths[member]
    video = videos[member]
    width = query.shape[1]
    gains = gain[...]
    sources = []
    for step in range(GROUP):
        sources.append(slot_for(store_map, member ^ step, member))
    source_of = []
    for b in range(SLOT_DEV):
        source = jnp.int32(-1)
        for step in range(GROUP):
            source = jnp.where(sources[step][1] == b, step, source)
        source_of.append(source)
    own_slot = sources[0][0]
    place = {1: 0, 3: 1, 2: 2}

    for b in range(SLOT_DEV):
        source = source_of[b]
        at = jnp.where(source == 1, place[1], jnp.where(source == 3, place[3], place[2]))
        at = pl.multiple_of(at * BLK, BLK)
        here = pl.multiple_of(jnp.maximum(own_slot, 0) * BLK, BLK)

        @pl.when(source == 0)
        def _():
            norm_into(
                stored[0, pl.ds(here, BLK), :], stored[1, pl.ds(here, BLK), :], gains, normed, b * BLK, BLK
            )

        @pl.when(source > 0)
        def _():
            norm_into(
                arrived[0, pl.ds(at, BLK), :], arrived[1, pl.ds(at, BLK), :], gains, normed, b * BLK, BLK
            )

        @pl.when(source < 0)
        def _():
            normed[b * BLK : (b + 1) * BLK, :] = jnp.zeros((BLK, normed.shape[1]), BF16)

    norm_into(stored[0, STORED:, :], stored[1, STORED:, :], gains, normed, CLIP_ROWS, PAD)

    tile = 256
    for which, out in ((0, query), (1, keys), (2, values)):
        for j in range(0, width, tile):
            got = jnp.dot(normed[...], w_qkv[which, :, j : j + tile], preferred_element_type=F32)
            if which == 0:
                got = got * HEAD_DIM ** (-0.5)
            out[: CLIP_ROWS + PAD, j : j + tile] = got.astype(BF16)
    for out in (keys, values):
        out[CLIP_ROWS + PAD :, :] = jnp.zeros((BLK - PAD, width), BF16)
    context[...] = jnp.zeros_like(context)

    lane = lax.broadcasted_iota(jnp.int32, (BLK, BLK), 1)
    low = lane < HEAD_DIM
    lane2 = lax.broadcasted_iota(jnp.int32, (2 * BLK, BLK), 1)
    nt = (((1,), (1,)), ((), ()))

    def token_block(b, first, count, source):
        start = pl.multiple_of(first * BLK, BLK)
        at = pl.multiple_of(b * BLK, BLK)
        for p in range(width // BLK):
            cols = slice(p * BLK, (p + 1) * BLK)
            q = query[pl.ds(at, BLK), cols]
            both = jnp.concatenate(
                [jnp.where(low, q, jnp.zeros_like(q)), jnp.where(low, jnp.zeros_like(q), q)], axis=0
            )
            seen = keys[pl.ds(start, count * BLK), cols]
            s = lax.dot_general(both, seen, nt, preferred_element_type=F32)
            se = lax.dot_general(both, keys[CLIP_ROWS:, cols], nt, preferred_element_type=F32)
            se = jnp.where(lane2 < NB, se, -1e30)
            top = se
            for k in range(count):
                top = jnp.maximum(top, s[:, k * BLK : (k + 1) * BLK])
            top = jnp.max(top, axis=-1, keepdims=True)
            e = jnp.exp(s - top).astype(BF16)
            ee = jnp.exp(se - top).astype(BF16)
            v = values[pl.ds(start, count * BLK), cols]
            v = jnp.concatenate([v, jnp.ones_like(v)], axis=1)
            ve = values[CLIP_ROWS:, cols]
            ve = jnp.concatenate([ve, jnp.ones_like(ve)], axis=1)
            o = jnp.dot(e, v, preferred_element_type=F32) + jnp.dot(ee, ve, preferred_element_type=F32)
            top_part = jnp.where(low, o[:BLK, :BLK], o[BLK:, :BLK])
            total = jnp.where(low, o[:BLK, BLK:], o[BLK:, BLK:])
            context[source, :, cols] = (top_part / total).astype(BF16)

    for b in range(SLOT_DEV):
        is_video = b < video
        first = jnp.where(is_video, 0, video)
        seen = jnp.where(is_video, video, length - video)
        for count in range(1, SLOT_DEV):

            @pl.when((b < length) & (seen == count))
            def _():
                token_block(b, first, count, jnp.maximum(source_of[b], 0))

    heads = width // HEAD_DIM
    sub = 8
    qe = query[CLIP_ROWS : CLIP_ROWS + PAD, :].astype(F32)[:sub]
    qe = jnp.concatenate([qe] * heads, axis=0)
    row_head = lax.broadcasted_iota(jnp.int32, (heads * sub, width), 0) // sub
    col_head = lax.broadcasted_iota(jnp.int32, (heads * sub, width), 1) // HEAD_DIM
    mine = row_head == col_head
    qe = jnp.where(mine, qe, 0.0).astype(BF16)
    s = lax.dot_general(qe, keys[...], nt, preferred_element_type=F32)
    col = lax.broadcasted_iota(jnp.int32, s.shape, 1)
    bottle = (col >= CLIP_ROWS) & (col < CLIP_ROWS + NB)
    parts = []
    for allowed in (
        bottle | (col < video * BLK),
        bottle | ((col >= video * BLK) & (col < length * BLK)),
    ):
        masked = jnp.where(allowed, s, -1e30)
        e = jnp.exp(masked - jnp.max(masked, axis=-1, keepdims=True))
        parts.append((e / jnp.sum(e, axis=-1, keepdims=True)).astype(BF16))
    o = jnp.dot(jnp.concatenate(parts, axis=0), values[...], preferred_element_type=F32)
    o = 0.5 * (o[: heads * sub] + o[heads * sub :])
    o = jnp.where(mine, o, 0.0)
    total = o[:sub]
    for h in range(1, heads):
        total = total + o[h * sub : (h + 1) * sub]
    own[BLK:, :] = jnp.concatenate([total, jnp.zeros_like(total)], axis=0).astype(BF16)
    own[:BLK, :] = context[0]
    near[...] = context[1]
    far[...] = context[2]
    across[...] = context[3]


def feed_kernel(
    store_map,
    stored,
    own,
    arrived,
    w_out,
    gain,
    w_up,
    w_down,
    base,
    send,
    context,
    after,
    normed,
    active,
):
    member = lax.axis_index("clip")
    core = lax.axis_index("mp")
    half = base.shape[1]
    for s in range(STORE_DEV):
        entry = store_map[member, s]
        step = jnp.where(entry >= 0, (entry // SLOT_DEV) ^ member, -1)
        at = jnp.where(step == 1, 0, jnp.where(step == 3, 1, 2))
        at = pl.multiple_of(at * BLK, BLK)
        rows = slice(s * BLK, (s + 1) * BLK)

        @pl.when(step == 0)
        def _():
            context[rows, :half] = own[0, :BLK, :]
            context[rows, half:] = own[1, :BLK, :]

        @pl.when(step > 0)
        def _():
            context[rows, :half] = arrived[0, pl.ds(at, BLK), :]
            context[rows, half:] = arrived[1, pl.ds(at, BLK), :]

        @pl.when(step < 0)
        def _():
            context[rows, :] = jnp.zeros((BLK, 2 * half), BF16)

    context[STORED:, :half] = own[0, BLK:, :]
    context[STORED:, half:] = own[1, BLK:, :]

    tile = 256
    for j in range(0, 2 * half, tile):
        got = jnp.dot(context[:, :half], w_out[0, :, j : j + tile], preferred_element_type=F32)
        got = got + jnp.dot(context[:, half:], w_out[1, :, j : j + tile], preferred_element_type=F32)
        side, off = divmod(j, half)
        got = got + stored[side, :, off : off + tile].astype(F32)
        after[:, j : j + tile] = got.astype(BF16)
    gains = gain[...]
    for r in range(0, ROWS, 80):
        norm_into(after[r : r + 80, :half], after[r : r + 80, half:], gains, normed, r, 80)
    hidden = w_up.shape[1]
    for j in range(0, hidden, tile):
        got = jnp.dot(normed[...], w_up[:, j : j + tile], preferred_element_type=F32)
        active[:, j : j + tile] = jax.nn.gelu(got, approximate=True).astype(BF16)
    for j in range(0, half, tile):
        mine = pl.multiple_of(core * half + j, tile)
        other = pl.multiple_of((1 - core) * half + j, tile)
        got = jnp.dot(active[...], w_down[:, pl.ds(other, tile)], preferred_element_type=F32)
        send[:, j : j + tile] = got.astype(BF16)
        got = jnp.dot(active[...], w_down[:, pl.ds(mine, tile)], preferred_element_type=F32)
        base[:, j : j + tile] = got + after[:, pl.ds(mine, tile)].astype(F32)


def finish_kernel(store_map, base, sums, mixed, merged):
    member = lax.axis_index("clip")
    core = lax.axis_index("mp")
    other = 1 - core
    for s in range(STORE_DEV):
        rows = slice(s * BLK, (s + 1) * BLK)
        got = base[rows, :] + sums[other, rows, :].astype(F32)
        keep = store_map[member, s] >= 0
        mixed[s] = jnp.where(keep, got, 0.0).astype(BF16)
    got = base[STORED:, :] + sums[other, STORED:, :].astype(F32)
    merged[0] = got[:NB].astype(BF16)


def body(
    tokens,
    bottleneck,
    clip_lengths,
    video_blocks,
    store_map,
    norm1_gain,
    w_qkv,
    w_out,
    norm2_gain,
    w_up,
    w_down,
):
    width = tokens.shape[2]
    model = 2 * width
    heads_width = w_qkv.shape[2]
    hidden = w_up.shape[1]
    gain1 = norm1_gain.reshape(1, model)
    gain2 = norm2_gain.reshape(1, model)
    block = spec((BLK, width))
    w_out_all = lax.all_gather(w_out, "mp", axis=0)

    near, across, far, stored = pl.pallas_call(
        pack_kernel,
        name="pack",
        out_shape=(block, block, block, spec((ROWS, width))),
        in_specs=[SMEM, VMEM, VMEM],
        out_specs=(VMEM,) * 4,
    )(store_map, tokens, bottleneck)
    across = partner(across, 3)
    near = partner(near, 1)
    far = partner(far, 2)
    stored_all = lax.all_gather(stored, "mp", axis=0)
    arrived = lax.all_gather(jnp.concatenate([near, across, far], axis=0), "mp", axis=0)

    near, across, far, own = pl.pallas_call(
        attend_kernel,
        name="attend",
        out_shape=(block, block, block, spec((BLK + PAD, width))),
        in_specs=[SMEM, SMEM, SMEM, VMEM, VMEM, VMEM, VMEM],
        out_specs=(VMEM,) * 4,
        scratch_shapes=[
            pltpu.VMEM((CLIP_ROWS + PAD, model), BF16),
            pltpu.VMEM((CLIP_ROWS + BLK, heads_width), BF16),
            pltpu.VMEM((CLIP_ROWS + BLK, heads_width), BF16),
            pltpu.VMEM((CLIP_ROWS + BLK, heads_width), BF16),
            pltpu.VMEM((GROUP, BLK, heads_width), BF16),
        ],
        compiler_params=pltpu.CompilerParams(vmem_limit_bytes=24 << 20),
        cost_estimate=pl.CostEstimate(flops=2500000000, bytes_accessed=6000000, transcendentals=3000000),
    )(store_map, clip_lengths, video_blocks, stored_all, arrived, gain1, w_qkv)
    across = partner(across, 3)
    near = partner(near, 1)
    far = partner(far, 2)
    own_all = lax.all_gather(own, "mp", axis=0)
    arrived = lax.all_gather(jnp.concatenate([near, across, far], axis=0), "mp", axis=0)

    base, send = pl.pallas_call(
        feed_kernel,
        name="feed",
        out_shape=(spec((ROWS, width), F32), spec((ROWS, width))),
        in_specs=[SMEM] + [VMEM] * 7,
        out_specs=(VMEM,) * 2,
        scratch_shapes=[
            pltpu.VMEM((ROWS, model), BF16),
            pltpu.VMEM((ROWS, model), BF16),
            pltpu.VMEM((ROWS, model), BF16),
            pltpu.VMEM((ROWS, hidden), BF16),
        ],
        compiler_params=pltpu.CompilerParams(vmem_limit_bytes=32 << 20),
        cost_estimate=pl.CostEstimate(flops=4100000000, bytes_accessed=14000000, transcendentals=820000),
    )(store_map, stored_all, own_all, arrived, w_out_all, gain2, w_up, w_down)
    sums = lax.all_gather(send, "mp", axis=0)

    mixed, merged = pl.pallas_call(
        finish_kernel,
        name="finish",
        out_shape=(spec(tokens.shape), spec(bottleneck.shape)),
        in_specs=[SMEM, VMEM, VMEM],
        out_specs=(VMEM,) * 2,
    )(store_map, base, sums)
    return mixed, merged


def solution(mesh):
    placed = (
        P("clip", None, "mp"),
        P("clip", None, "mp"),
        P(),
        P(),
        P(),
        P(),
        P(None, None, "mp"),
        P("mp", None),
        P(),
        P(None, "mp"),
        P("mp", None),
    )
    return jax.shard_map(
        body,
        mesh=mesh,
        in_specs=placed,
        out_specs=(P("clip", None, "mp"), P("clip", None, "mp")),
        check_vma=False,
    )
```

profile of v0, /device:TPU:1, one launch (start us, length us, event | category | flops | bytes accessed | tf_op | source)
XLA Modules:
  0.0 77.9 jit_solution(8926579743690617311)
XLA Ops:
  7.2 0.0 copy-start.7
  7.2 0.0 copy-start.10
  7.2 0.0 copy-start.9
  7.2 0.0 all-gather.8.cloned.1.call-start
  7.2 0.7 all-gather.8.cloned.1.call-update
  7.9 1.4 %copy.16.store_map = s32[128,3]{1,0:T(8,128)} copy(s32[128,3]{0,1:T(4,128)} %param.15) | data formatting | bytes 3072 | tf_op args[4]
  9.3 2.8 %pack.1 = (bf16[128,512]{1,0:T(8,128)(2,1)}, bf16[128,512]{1,0:T(8,128)(2,1)}, bf16[128,512]{1,0:T(8,128)(2,1)}, bf16[400,512]{1,0:T(8,128)(2,1)}) custom-call(s32[128,3]{1,0:T(8,128)} %copy.16.store_map, bf16[3,128,512]{2,1,0:T(8,128)(2,1)} %tokens.1, bf16[1,4,512]{2,1,0:T(4,128)(2,1)} %extra.1), custom_call_target="tpu_custom_call" | custom-call | tf_op jit(solution)/shard_map/pack/pallas_call | solution.py:329
  12.1 2.0 %collective-permute-start = (bf16[128,512]{1,0:T(8,128)(2,1)}, bf16[128,512]{1,0:T(8,128)(2,1)S(1)}, u32[]{:S(2)}, u32[]{:S(2)}) collective-permute-start(bf16[128,512]{1,0:T(8,128)(2,1)} %get-tuple-element.13), channel_id=1, source_target_pairs={{0,2},{2,0},{4,6},{6,4},{8,10},{10,8},{12,14},{14,12},{16,18},{18,... | collective-permute-start | bytes 393224 | tf_op jit(solution)/shard_map/ppermute | solution.py:32
  14.1 1.8 %collective-permute-start.1 = (bf16[128,512]{1,0:T(8,128)(2,1)}, bf16[128,512]{1,0:T(8,128)(2,1)S(1)}, u32[]{:S(2)}, u32[]{:S(2)}) collective-permute-start(bf16[128,512]{1,0:T(8,128)(2,1)} %get-tuple-element.14), channel_id=1, source_target_pairs={{0,6},{2,4},{4,2},{6,0},{8,14},{10,12},{12,10},{14,8},{16,22},{18,... | collective-permute-start | bytes 393224 | tf_op jit(solution)/shard_map/ppermute | solution.py:32
  15.9 0.6 collective-permute-start.2
  16.6 5.1 %all-gather = bf16[800,512]{1,0:T(8,128)(2,1)S(1)} all-gather(bf16[400,512]{1,0:T(8,128)(2,1)} %get-tuple-element.12), channel_id=2, replica_groups=mesh['clip'=128,'mp'=2] {'mp'}, dimensions={0}, use_global_device_ids=true | all-gather | bytes 1228800 | tf_op jit(solution)/shard_map/all_gather | solution.py:339
  21.6 0.0 collective-permute-done
  21.6 0.0 collective-permute-done.1
  21.6 0.8 collective-permute-done.2
  22.4 4.1 %all-gather.1 = bf16[768,512]{1,0:T(8,128)(2,1)S(1)} all-gather(bf16[384,512]{1,0:T(8,128)(2,1)S(1)} %pad_maximum_fusion), channel_id=3, replica_groups=mesh['clip'=128,'mp'=2] {'mp'}, dimensions={0}, use_global_device_ids=true | all-gather | bytes 1179648 | tf_op jit(solution)/shard_map/all_gather | solution.py:340
  26.6 0.0 copy-done.7
  26.6 0.0 copy-done.10
  26.6 0.0 copy-done.9
  26.6 0.0 copy-start.1
  26.6 0.8 %copy-done.1 = s32[128,3]{1,0:T(8,128)S(1)} copy-done((s32[128,3]{1,0:T(8,128)S(1)}, s32[128,3]{1,0:T(8,128)}, u32[]{:S(2)}) %copy-start.1) | copy-done | bytes 1560
  27.4 0.0 copy-start.5
  27.4 2.2 %copy-done.5 = bf16[3,1024,512]{2,1,0:T(8,128)(2,1)S(1)} copy-done((bf16[3,1024,512]{2,1,0:T(8,128)(2,1)S(1)}, bf16[3,1024,512]{2,1,0:T(8,128)(2,1)}, u32[]{:S(2)}) %copy-start.5) | copy-done | bytes 3145752
  29.6 0.0 copy-start.2
  29.6 0.0 copy-start.8
  29.6 7.2 %attend.1 = (bf16[128,512]{1,0:T(8,128)(2,1)S(1)}, bf16[128,512]{1,0:T(8,128)(2,1)S(1)}, bf16[128,512]{1,0:T(8,128)(2,1)S(1)}, bf16[144,512]{1,0:T(8,128)(2,1)S(1)}) custom-call(s32[128,3]{1,0:T(8,128)S(1)} %copy-done.1, s32[128]{0:T(128)S(1)} %copy-done.9, s32[128]{0:T(128)S(1)} %copy-done.10, bf16[2,400,512]{2,1,0:T(8,128)(2,1)S(1)} %bitcast.8, ...), custom_call_target="tpu_custom_call" | custom-call | flops 2500000000 | bytes 6000000 | tf_op jit(solution)/shard_map/attend/pallas_call | solution.py:342
  36.8 2.1 %collective-permute-start.3 = (bf16[128,512]{1,0:T(8,128)(2,1)S(1)}, bf16[128,512]{1,0:T(8,128)(2,1)S(1)}, u32[]{:S(2)}, u32[]{:S(2)}) collective-permute-start(bf16[128,512]{1,0:T(8,128)(2,1)S(1)} %get-tuple-element.17), channel_id=1, source_target_pairs={{0,2},{2,0},{4,6},{6,4},{8,10},{10,8},{12,14},{14,12},{16,18},{18,... | collective-permute-start | bytes 393224 | tf_op jit(solution)/shard_map/ppermute | solution.py:32
  38.9 4.0 %collective-permute-start.4 = (bf16[128,512]{1,0:T(8,128)(2,1)S(1)}, bf16[128,512]{1,0:T(8,128)(2,1)S(1)}, u32[]{:S(2)}, u32[]{:S(2)}) collective-permute-start(bf16[128,512]{1,0:T(8,128)(2,1)S(1)} %get-tuple-element.18), channel_id=1, source_target_pairs={{0,6},{2,4},{4,2},{6,0},{8,14},{10,12},{12,10},{14,8},{16,22},{18,... | collective-permute-start | bytes 393224 | tf_op jit(solution)/shard_map/ppermute | solution.py:32
  42.9 0.0 collective-permute-start.5
  42.9 2.6 %all-gather.2 = bf16[288,512]{1,0:T(8,128)(2,1)S(1)} all-gather(bf16[144,512]{1,0:T(8,128)(2,1)S(1)} %get-tuple-element.16), channel_id=4, replica_groups=mesh['clip'=128,'mp'=2] {'mp'}, dimensions={0}, use_global_device_ids=true | all-gather | bytes 442368 | tf_op jit(solution)/shard_map/all_gather | solution.py:361
  45.5 0.0 collective-permute-done.3
  45.5 3.1 %collective-permute-done.4 = bf16[128,512]{1,0:T(8,128)(2,1)S(1)} collective-permute-done((bf16[128,512]{1,0:T(8,128)(2,1)S(1)}, bf16[128,512]{1,0:T(8,128)(2,1)S(1)}, u32[]{:S(2)}, u32[]{:S(2)}) %collective-permute-start.4) | collective-permute-done | bytes 131104 | tf_op jit(solution)/shard_map/ppermute | solution.py:32
  48.6 0.0 collective-permute-done.5
  48.6 3.7 %all-gather.3 = bf16[768,512]{1,0:T(8,128)(2,1)S(1)} all-gather(bf16[384,512]{1,0:T(8,128)(2,1)S(1)} %pad_maximum_fusion.1), channel_id=5, replica_groups=mesh['clip'=128,'mp'=2] {'mp'}, dimensions={0}, use_global_device_ids=true | all-gather | bytes 1179648 | tf_op jit(solution)/shard_map/all_gather | solution.py:362
  52.3 0.0 all-gather.8.cloned.1.call-done
  52.4 0.0 copy-done.2
  52.4 0.0 copy-done.8
  52.4 0.0 copy-start.3
  52.4 2.2 %copy-done.3 = bf16[1024,2048]{1,0:T(8,128)(2,1)S(1)} copy-done((bf16[1024,2048]{1,0:T(8,128)(2,1)S(1)}, bf16[1024,2048]{1,0:T(8,128)(2,1)}, u32[]{:S(2)}) %copy-start.3) | copy-done | bytes 4194328
  54.5 0.0 copy-start.4
  54.5 2.2 %copy-done.4 = bf16[2048,1024]{1,0:T(8,128)(2,1)S(1)} copy-done((bf16[2048,1024]{1,0:T(8,128)(2,1)S(1)}, bf16[2048,1024]{1,0:T(8,128)(2,1)}, u32[]{:S(2)}) %copy-start.4) | copy-done | bytes 4194328
  56.7 0.0 copy-start.6
  56.7 1.6 %copy-done.6 = bf16[1024,1024]{1,0:T(8,128)(2,1)S(1)} copy-done((bf16[1024,1024]{1,0:T(8,128)(2,1)S(1)}, bf16[1024,1024]{1,0:T(8,128)(2,1)}, u32[]{:S(2)}) %copy-start.6) | copy-done | bytes 2097176
  58.3 6.8 %feed.1 = (f32[400,512]{1,0:T(8,128)S(1)}, bf16[400,512]{1,0:T(8,128)(2,1)S(1)}) custom-call(s32[128,3]{1,0:T(8,128)S(1)} %copy-done.2, bf16[2,400,512]{2,1,0:T(8,128)(2,1)S(1)} %bitcast.9, bf16[2,144,512]{2,1,0:T(8,128)(2,1)S(1)} %bitcast.12, bf16[2,384,512]{2,1,0:T(8,128)(2,1)S(1)} %bitcast.10, bf16[2,512,1024]{2,1,0:T(8,128)(2,1)S(1)} %bitcast.13, ...), custom_call_target="tpu_custom_call" | custom-call | flops 4100000000 | bytes 14000000 | tf_op jit(solution)/shard_map/feed/pallas_call | solution.py:364
  65.1 0.0 copy-start
  65.1 0.9 %copy-done = f32[400,512]{1,0:T(8,128)} copy-done((f32[400,512]{1,0:T(8,128)}, f32[400,512]{1,0:T(8,128)S(1)}, u32[]{:S(2)}) %copy-start) | copy-done | bytes 819224
  66.0 2.5 %all-gather.5 = bf16[800,512]{1,0:T(8,128)(2,1)} all-gather(bf16[400,512]{1,0:T(8,128)(2,1)S(1)} %get-tuple-element.21), channel_id=7, replica_groups=mesh['clip'=128,'mp'=2] {'mp'}, dimensions={0}, use_global_device_ids=true | all-gather | bytes 1228800 | tf_op jit(solution)/shard_map/all_gather | solution.py:379
  68.5 2.6 %finish.1 = (bf16[3,128,512]{2,1,0:T(8,128)(2,1)}, bf16[1,4,512]{2,1,0:T(4,128)(2,1)}) custom-call(s32[128,3]{1,0:T(8,128)} %copy.16.store_map, f32[400,512]{1,0:T(8,128)} %copy-done, bf16[2,400,512]{2,1,0:T(8,128)(2,1)} %bitcast.16), custom_call_target="tpu_custom_call" | custom-call | tf_op jit(solution)/shard_map/finish/pallas_call | solution.py:381
  (2 shorter events, 0.1 us)
Async XLA Ops:
  7.2 19.4 %copy-start.7 = (f32[1024]{0:T(1024)S(1)}, f32[1024]{0:T(1024)}, u32[]{:S(2)}) copy-start(f32[1024]{0:T(1024)} %param.16) | copy-start | bytes 12292
  7.2 19.4 %copy-start.10 = (s32[128]{0:T(128)S(1)}, s32[128]{0:T(128)}, u32[]{:S(2)}) copy-start(s32[128]{0:T(128)} %videos.1) | copy-start | bytes 1540
  7.2 19.4 %copy-start.9 = (s32[128]{0:T(128)S(1)}, s32[128]{0:T(128)}, u32[]{:S(2)}) copy-start(s32[128]{0:T(128)} %lengths.1) | copy-start | bytes 1540
  7.2 45.2 %all-gather.8.cloned.1.call-start = ((), (), s32[]{:S(2)}) async-start(), calls=%async_computation | async-start | bytes 3145728 | tf_op jit(solution)/shard_map/all_gather | solution.py:327
  12.1 9.6 %collective-permute-start = (bf16[128,512]{1,0:T(8,128)(2,1)}, bf16[128,512]{1,0:T(8,128)(2,1)S(1)}, u32[]{:S(2)}, u32[]{:S(2)}) collective-permute-start(bf16[128,512]{1,0:T(8,128)(2,1)} %get-tuple-element.13), channel_id=1, source_target_pairs={{0,2},{2,0},{4,6},{6,4},{8,10},{10,8},{12,14},{14,12},{16,18},{18,... | collective-permute-start | bytes 393224 | tf_op jit(solution)/shard_map/ppermute | solution.py:32
  14.1 7.5 %collective-permute-start.1 = (bf16[128,512]{1,0:T(8,128)(2,1)}, bf16[128,512]{1,0:T(8,128)(2,1)S(1)}, u32[]{:S(2)}, u32[]{:S(2)}) collective-permute-start(bf16[128,512]{1,0:T(8,128)(2,1)} %get-tuple-element.14), channel_id=1, source_target_pairs={{0,6},{2,4},{4,2},{6,0},{8,14},{10,12},{12,10},{14,8},{16,22},{18,... | collective-permute-start | bytes 393224 | tf_op jit(solution)/shard_map/ppermute | solution.py:32
  15.9 6.5 %collective-permute-start.2 = (bf16[128,512]{1,0:T(8,128)(2,1)}, bf16[128,512]{1,0:T(8,128)(2,1)S(1)}, u32[]{:S(2)}, u32[]{:S(2)}) collective-permute-start(bf16[128,512]{1,0:T(8,128)(2,1)} %get-tuple-element.15), channel_id=1, source_target_pairs={{0,4},{2,6},{4,0},{6,2},{8,12},{10,14},{12,8},{14,10},{16,20},{18,... | collective-permute-start | bytes 393224 | tf_op jit(solution)/shard_map/ppermute | solution.py:32
  26.6 0.8 %copy-start.1 = (s32[128,3]{1,0:T(8,128)S(1)}, s32[128,3]{1,0:T(8,128)}, u32[]{:S(2)}) copy-start(s32[128,3]{1,0:T(8,128)} %copy.16.store_map) | copy-start | bytes 4612
  27.4 2.2 %copy-start.5 = (bf16[3,1024,512]{2,1,0:T(8,128)(2,1)S(1)}, bf16[3,1024,512]{2,1,0:T(8,128)(2,1)}, u32[]{:S(2)}) copy-start(bf16[3,1024,512]{2,1,0:T(8,128)(2,1)} %w_qkv.1) | copy-start | bytes 9437188
  29.6 22.8 %copy-start.2 = (s32[128,3]{1,0:T(8,128)S(1)}, s32[128,3]{1,0:T(8,128)}, u32[]{:S(2)}) copy-start(s32[128,3]{1,0:T(8,128)} %copy.16.store_map) | copy-start | bytes 4612
  29.6 22.8 %copy-start.8 = (f32[1024]{0:T(1024)S(1)}, f32[1024]{0:T(1024)}, u32[]{:S(2)}) copy-start(f32[1024]{0:T(1024)} %param.19) | copy-start | bytes 12292
  36.8 8.7 %collective-permute-start.3 = (bf16[128,512]{1,0:T(8,128)(2,1)S(1)}, bf16[128,512]{1,0:T(8,128)(2,1)S(1)}, u32[]{:S(2)}, u32[]{:S(2)}) collective-permute-start(bf16[128,512]{1,0:T(8,128)(2,1)S(1)} %get-tuple-element.17), channel_id=1, source_target_pairs={{0,2},{2,0},{4,6},{6,4},{8,10},{10,8},{12,14},{14,12},{16,18},{18,... | collective-permute-start | bytes 393224 | tf_op jit(solution)/shard_map/ppermute | solution.py:32
  38.9 9.7 %collective-permute-start.4 = (bf16[128,512]{1,0:T(8,128)(2,1)S(1)}, bf16[128,512]{1,0:T(8,128)(2,1)S(1)}, u32[]{:S(2)}, u32[]{:S(2)}) collective-permute-start(bf16[128,512]{1,0:T(8,128)(2,1)S(1)} %get-tuple-element.18), channel_id=1, source_target_pairs={{0,6},{2,4},{4,2},{6,0},{8,14},{10,12},{12,10},{14,8},{16,22},{18,... | collective-permute-start | bytes 393224 | tf_op jit(solution)/shard_map/ppermute | solution.py:32
  42.9 5.7 %collective-permute-start.5 = (bf16[128,512]{1,0:T(8,128)(2,1)S(1)}, bf16[128,512]{1,0:T(8,128)(2,1)S(1)}, u32[]{:S(2)}, u32[]{:S(2)}) collective-permute-start(bf16[128,512]{1,0:T(8,128)(2,1)S(1)} %get-tuple-element.19), channel_id=1, source_target_pairs={{0,4},{2,6},{4,0},{6,2},{8,12},{10,14},{12,8},{14,10},{16,20},{18,... | collective-permute-start | bytes 393224 | tf_op jit(solution)/shard_map/ppermute | solution.py:32
  52.4 2.2 %copy-start.3 = (bf16[1024,2048]{1,0:T(8,128)(2,1)S(1)}, bf16[1024,2048]{1,0:T(8,128)(2,1)}, u32[]{:S(2)}) copy-start(bf16[1024,2048]{1,0:T(8,128)(2,1)} %w_up.1) | copy-start | bytes 12582916
  54.5 2.2 %copy-start.4 = (bf16[2048,1024]{1,0:T(8,128)(2,1)S(1)}, bf16[2048,1024]{1,0:T(8,128)(2,1)}, u32[]{:S(2)}) copy-start(bf16[2048,1024]{1,0:T(8,128)(2,1)} %w_down.1) | copy-start | bytes 12582916
  56.7 1.6 %copy-start.6 = (bf16[1024,1024]{1,0:T(8,128)(2,1)S(1)}, bf16[1024,1024]{1,0:T(8,128)(2,1)}, u32[]{:S(2)}) copy-start(bf16[1024,1024]{1,0:T(8,128)(2,1)} %all-gather.8.cloned.1.call-done) | copy-start | bytes 6291460
  65.1 0.9 %copy-start = (f32[400,512]{1,0:T(8,128)}, f32[400,512]{1,0:T(8,128)S(1)}, u32[]{:S(2)}) copy-start(f32[400,512]{1,0:T(8,128)S(1)} %get-tuple-element.20.base) | copy-start | bytes 2457604
Sparse Core Ops, SparseCore 0:
  9.8 20.4 all-gather.7
where the time goes:
time: 78.7 us; the launch traced here: 77.9 us
  Pallas kernels  19.3 us (25%)
  blocking collectives  18 us (23%)
  between operations  14.1 us (18%)
  local copies, waits for them, and re-layouts  11.3 us (14%)
  starting transfers between devices  10.6 us (13%)
  waiting for transfers between devices  4.57 us (6%)
    unnamed x23, local copies, waits for them, and re-layouts  11.3 us
    ppermute x6, starting transfers between devices, partner(): lax.ppermute(x, 'clip', [(i, i ^ step) for i in range(lax.axis_size('clip...  10.6 us
    all_gather x2, blocking collectives, body(): lax.all_gather(jnp.concatenate([near, across, far], axis=0), 'mp', axis=0)  7.82 us
    pallas_call x1, Pallas kernels, body(): pl.pallas_call(attend_kernel, name='attend', out_shape=(block, block, blo...  7.21 us
    pallas_call x1, Pallas kernels, body(): pl.pallas_call(feed_kernel, name='feed', out_shape=(spec((ROWS, width), F...  6.77 us
    all_gather x1, blocking collectives, body(): stored_all = lax.all_gather(stored, 'mp', axis=0)  5.06 us
    ppermute x6, waiting for transfers between devices, partner(): lax.ppermute(x, 'clip', [(i, i ^ step) for i in range(lax.axis_size('clip...  3.89 us
    pallas_call x1, Pallas kernels, body(): pl.pallas_call(pack_kernel, name='pack', out_shape=(block, block, block,...  2.75 us
  transfers between devices with their start and end apart: 7, of which 2 were waited for; matrix products, arithmetic and copies ran while one was open for 2% of the time, Pallas kernels for 13%

commit v1 on v0

v1 whole, which is shorter than its diff:
```python
import jax
import jax.numpy as jnp
from jax import lax
from jax.experimental import pallas as pl
from jax.experimental.pallas import tpu as pltpu
from jax.sharding import PartitionSpec as P

HEAD_DIM = 64
BLK = 128
NB = 4
SLOT_DEV = 4
STORE_DEV = 3
GROUP = 4
PAD = 16
STORED = STORE_DEV * BLK
ROWS = STORED + PAD
CLIP_ROWS = SLOT_DEV * BLK
BF16 = jnp.bfloat16
F32 = jnp.float32

VMEM = pl.BlockSpec(memory_space=pltpu.VMEM)
HBM = pl.BlockSpec(memory_space=pltpu.HBM)
DMA = pltpu.SemaphoreType.DMA
SMEM = pl.BlockSpec(memory_space=pltpu.SMEM)


def spec(shape, dtype=BF16):
    return jax.ShapeDtypeStruct(shape, dtype)


def partner(x, step):
    return lax.ppermute(x, "clip", [(i, i ^ step) for i in range(lax.axis_size("clip"))])


def slot_for(store_map, device, owner):
    slot = jnp.int32(-1)
    block = jnp.int32(-1)
    for s in range(STORE_DEV):
        entry = store_map[s, device]
        hit = (entry >= 0) & (entry // SLOT_DEV == owner)
        slot = jnp.where(hit, s, slot)
        block = jnp.where(hit, entry % SLOT_DEV, block)
    return slot, block


def norm_into(x0, x1, gain, out, at, rows):
    half = x0.shape[1]
    x0 = x0.astype(F32)
    x1 = x1.astype(F32)
    scale = 1.0 / (2 * half)
    mean = (jnp.sum(x0, axis=-1, keepdims=True) + jnp.sum(x1, axis=-1, keepdims=True)) * scale
    x0 = x0 - mean
    x1 = x1 - mean
    moment = (
        jnp.sum(x0 * x0, axis=-1, keepdims=True) + jnp.sum(x1 * x1, axis=-1, keepdims=True)
    ) * scale
    inv = lax.rsqrt(moment + 1e-05)
    out[pl.ds(at, rows), :half] = (x0 * inv * gain[:, :half]).astype(BF16)
    out[pl.ds(at, rows), half:] = (x1 * inv * gain[:, half:]).astype(BF16)


def pack_kernel(slots, tokens, extra, near, across, far, stored, store_map, few, tail, sems):
    member = lax.axis_index("clip")
    load_map = pltpu.make_async_copy(slots, store_map, sems.at[0])
    load_few = pltpu.make_async_copy(extra, few, sems.at[1])
    load_map.start()
    load_few.start()
    copies = [
        pltpu.make_async_copy(tokens.at[s], stored.at[pl.ds(s * BLK, BLK), :], sems.at[2 + s])
        for s in range(STORE_DEV)
    ]
    load_map.wait()
    for k, (step, out) in enumerate(((1, near), (3, across), (2, far))):
        slot, _ = slot_for(store_map, member, member ^ step)
        copies.append(
            pltpu.make_async_copy(tokens.at[jnp.maximum(slot, 0)], out, sems.at[2 + STORE_DEV + k])
        )
    for copy in copies:
        copy.start()
    load_few.wait()
    width = stored.shape[1]
    tail[...] = jnp.concatenate(
        [few[0].astype(F32), jnp.zeros((PAD - NB, width), F32)], axis=0
    ).astype(BF16)
    last = pltpu.make_async_copy(tail, stored.at[pl.ds(STORED, PAD), :], sems.at[2 + 2 * STORE_DEV])
    last.start()
    for copy in copies + [last]:
        copy.wait()


def attend_kernel(
    slots,
    all_lengths,
    all_videos,
    stored,
    arrived,
    gain_in,
    w_qkv,
    near,
    across,
    far,
    own,
    normed,
    query,
    keys,
    values,
    context,
    weights,
    gain,
    store_map,
    lengths,
    videos,
    sems,
):
    member = lax.axis_index("clip")
    small = [
        pltpu.make_async_copy(x, y, sems.at[i])
        for i, (x, y) in enumerate(
            ((gain_in, gain), (slots, store_map), (all_lengths, lengths), (all_videos, videos))
        )
    ]
    loads = [pltpu.make_async_copy(w_qkv.at[i], weights.at[i], sems.at[4 + i]) for i in range(3)]
    for load in small + loads:
        load.start()
    width = query.shape[1]
    for load in small:
        load.wait()
    gains = gain[...]
    for k in range(GROUP - 1):
        rows = slice(k * BLK, (k + 1) * BLK)
        norm_into(arrived[0, rows, :], arrived[1, rows, :], gains, normed, k * BLK, BLK)
    norm_into(stored[0, STORED:, :], stored[1, STORED:, :], gains, normed, CLIP_ROWS, PAD)

    length = lengths[member]
    video = videos[member]
    own_slot, own_block = slot_for(store_map, member, member)
    here = pl.multiple_of(jnp.maximum(own_slot, 0) * BLK, BLK)
    norm_into(
        stored[0, pl.ds(here, BLK), :],
        stored[1, pl.ds(here, BLK), :],
        gains,
        normed,
        (GROUP - 1) * BLK,
        BLK,
    )
    block_at = [slot_for(store_map, member ^ step, member)[1] for step in (1, 3, 2)] + [own_block]
    source_of = []
    for b in range(SLOT_DEV):
        source = jnp.int32(0)
        for place, block in enumerate(block_at):
            source = jnp.where(block == b, place, source)
        source_of.append(source)
    row_at = [
        pl.multiple_of(jnp.where(block < 0, SLOT_DEV + 1, block) * BLK, BLK) for block in block_at
    ]

    tile = 256
    for which, out in ((0, query), (1, keys), (2, values)):
        loads[which].wait()
        for j in range(0, width, tile):
            got = jnp.dot(normed[...], weights[which, :, j : j + tile], preferred_element_type=F32)
            if which == 0:
                got = got * HEAD_DIM ** (-0.5)
            got = got.astype(BF16)
            for place in range(GROUP):
                out[pl.ds(row_at[place], BLK), j : j + tile] = got[place * BLK : (place + 1) * BLK]
            out[CLIP_ROWS : CLIP_ROWS + PAD, j : j + tile] = got[CLIP_ROWS:]
    for out in (keys, values):
        out[CLIP_ROWS + PAD : CLIP_ROWS + BLK, :] = jnp.zeros((BLK - PAD, width), BF16)
    for b in range(2, SLOT_DEV):

        @pl.when(b >= length)
        def _():
            values[b * BLK : (b + 1) * BLK, :] = jnp.zeros((BLK, width), BF16)

    context[...] = jnp.zeros_like(context)

    lane = lax.broadcasted_iota(jnp.int32, (BLK, BLK), 1)
    low = lane < HEAD_DIM
    lane2 = lax.broadcasted_iota(jnp.int32, (2 * BLK, BLK), 1)
    nt = (((1,), (1,)), ((), ()))

    def token_block(b, first, count, source):
        start = pl.multiple_of(first * BLK, BLK)
        at = pl.multiple_of(b * BLK, BLK)
        for p in range(width // BLK):
            cols = slice(p * BLK, (p + 1) * BLK)
            q = query[pl.ds(at, BLK), cols]
            both = jnp.concatenate(
                [jnp.where(low, q, jnp.zeros_like(q)), jnp.where(low, jnp.zeros_like(q), q)], axis=0
            )
            seen = keys[pl.ds(start, count * BLK), cols]
            s = lax.dot_general(both, seen, nt, preferred_element_type=F32)
            se = lax.dot_general(both, keys[CLIP_ROWS : CLIP_ROWS + BLK, cols], nt, preferred_element_type=F32)
            se = jnp.where(lane2 < NB, se, -1e30)
            top = se
            for k in range(count):
                top = jnp.maximum(top, s[:, k * BLK : (k + 1) * BLK])
            top = jnp.max(top, axis=-1, keepdims=True)
            e = jnp.exp(s - top).astype(BF16)
            ee = jnp.exp(se - top).astype(BF16)
            v = values[pl.ds(start, count * BLK), cols]
            v = jnp.concatenate([v, jnp.ones_like(v)], axis=1)
            ve = values[CLIP_ROWS : CLIP_ROWS + BLK, cols]
            ve = jnp.concatenate([ve, jnp.ones_like(ve)], axis=1)
            o = jnp.dot(e, v, preferred_element_type=F32) + jnp.dot(ee, ve, preferred_element_type=F32)
            top_part = jnp.where(low, o[:BLK, :BLK], o[BLK:, :BLK])
            total = jnp.where(low, o[:BLK, BLK:], o[BLK:, BLK:])
            context[source, :, cols] = (top_part / total).astype(BF16)

    for b in range(SLOT_DEV):
        is_video = b < video
        first = jnp.where(is_video, 0, video)
        seen = jnp.where(is_video, video, length - video)
        for count in range(1, SLOT_DEV):

            @pl.when((b < length) & (seen == count))
            def _():
                token_block(b, first, count, source_of[b])

    heads = width // HEAD_DIM
    sub = 8
    qe = query[CLIP_ROWS : CLIP_ROWS + PAD, :].astype(F32)[:sub]
    qe = jnp.concatenate([qe] * heads, axis=0)
    row_head = lax.broadcasted_iota(jnp.int32, (heads * sub, width), 0) // sub
    col_head = lax.broadcasted_iota(jnp.int32, (heads * sub, width), 1) // HEAD_DIM
    mine = row_head == col_head
    qe = jnp.where(mine, qe, 0.0).astype(BF16)
    s = lax.dot_general(qe, keys[: CLIP_ROWS + BLK, :], nt, preferred_element_type=F32)
    col = lax.broadcasted_iota(jnp.int32, s.shape, 1)
    bottle = (col >= CLIP_ROWS) & (col < CLIP_ROWS + NB)
    parts = []
    for allowed in (
        bottle | (col < video * BLK),
        bottle | ((col >= video * BLK) & (col < length * BLK)),
    ):
        masked = jnp.where(allowed, s, -1e30)
        e = jnp.exp(masked - jnp.max(masked, axis=-1, keepdims=True))
        parts.append((e / jnp.sum(e, axis=-1, keepdims=True)).astype(BF16))
    o = jnp.dot(jnp.concatenate(parts, axis=0), values[: CLIP_ROWS + BLK, :], preferred_element_type=F32)
    o = 0.5 * (o[: heads * sub] + o[heads * sub :])
    o = jnp.where(mine, o, 0.0)
    total = o[:sub]
    for h in range(1, heads):
        total = total + o[h * sub : (h + 1) * sub]
    own[BLK:, :] = jnp.concatenate([total, jnp.zeros_like(total)], axis=0).astype(BF16)
    near[...] = context[0]
    across[...] = context[1]
    far[...] = context[2]
    own[:BLK, :] = context[3]


def feed_kernel(
    store_map,
    stored,
    own,
    arrived,
    w_out,
    w_out_other,
    gain,
    w_up,
    w_down,
    base,
    send,
    context,
    after,
    normed,
    active,
    outs,
    ups,
    downs,
    sems,
):
    member = lax.axis_index("clip")
    core = lax.axis_index("mp")
    half = base.shape[1]
    hidden = w_up.shape[1]
    loads_out = [
        pltpu.make_async_copy(w_out, outs.at[0], sems.at[0]),
        pltpu.make_async_copy(w_out_other, outs.at[1], sems.at[1]),
    ]
    part = 512
    loads_up = [
        pltpu.make_async_copy(
            w_up.at[:, pl.ds(k * part, part)], ups.at[:, pl.ds(k * part, part)], sems.at[2 + k]
        )
        for k in range(hidden // part)
    ]
    loads_down = []
    for k, side in enumerate((1 - core, core)):
        loads_down.append(
            pltpu.make_async_copy(
                w_down.at[:, pl.ds(pl.multiple_of(side * half, half), half)],
                downs.at[k],
                sems.at[2 + hidden // part + k],
            )
        )
    for load in loads_out + loads_up + loads_down:
        load.start()
    sides = (core, 1 - core)
    for s in range(STORE_DEV):
        entry = store_map[s, member]
        step = jnp.where(entry >= 0, (entry // SLOT_DEV) ^ member, -1)
        at = jnp.where(step == 1, 0, jnp.where(step == 3, 1, 2))
        at = pl.multiple_of(at * BLK, BLK)
        rows = slice(s * BLK, (s + 1) * BLK)

        @pl.when(step == 0)
        def _():
            for k in range(2):
                context[k, rows, :] = own[sides[k], :BLK, :]

        @pl.when(step > 0)
        def _():
            for k in range(2):
                context[k, rows, :] = arrived[sides[k], pl.ds(at, BLK), :]

        @pl.when(step < 0)
        def _():
            for k in range(2):
                context[k, rows, :] = jnp.zeros((BLK, half), BF16)

    for k in range(2):
        context[k, STORED:, :] = own[sides[k], BLK:, :]

    tile = 256
    for load in loads_out:
        load.wait()
    for j in range(0, 2 * half, tile):
        got = jnp.dot(context[0], outs[0, :, j : j + tile], preferred_element_type=F32)
        got = got + jnp.dot(context[1], outs[1, :, j : j + tile], preferred_element_type=F32)
        side, off = divmod(j, half)
        got = got + stored[side, :, off : off + tile].astype(F32)
        after[:, j : j + tile] = got.astype(BF16)
    gains = gain[...]
    for r in range(0, ROWS, 80):
        norm_into(after[r : r + 80, :half], after[r : r + 80, half:], gains, normed, r, 80)
    for k, load in enumerate(loads_up):
        load.wait()
        for j in range(k * part, (k + 1) * part, tile):
            got = jnp.dot(normed[...], ups[:, j : j + tile], preferred_element_type=F32)
            active[:, j : j + tile] = jax.nn.gelu(got, approximate=True).astype(BF16)
    loads_down[0].wait()
    for j in range(0, half, tile):
        got = jnp.dot(active[...], downs[0, :, j : j + tile], preferred_element_type=F32)
        send[:, j : j + tile] = got.astype(BF16)
    loads_down[1].wait()
    for j in range(0, half, tile):
        mine = pl.multiple_of(core * half + j, tile)
        got = jnp.dot(active[...], downs[1, :, j : j + tile], preferred_element_type=F32)
        base[:, j : j + tile] = got + after[:, pl.ds(mine, tile)].astype(F32)


def finish_kernel(store_map, base, sums, mixed, merged):
    member = lax.axis_index("clip")
    core = lax.axis_index("mp")
    other = 1 - core
    for s in range(STORE_DEV):
        rows = slice(s * BLK, (s + 1) * BLK)
        got = base[rows, :] + sums[other, rows, :].astype(F32)
        keep = store_map[s, member] >= 0
        mixed[s] = jnp.where(keep, got, 0.0).astype(BF16)
    got = base[STORED:, :] + sums[other, STORED:, :].astype(F32)
    merged[0] = got[:NB].astype(BF16)


def body(
    tokens,
    bottleneck,
    clip_lengths,
    video_blocks,
    store_map,
    norm1_gain,
    w_qkv,
    w_out,
    norm2_gain,
    w_up,
    w_down,
):
    width = tokens.shape[2]
    model = 2 * width
    heads_width = w_qkv.shape[2]
    hidden = w_up.shape[1]
    gain1 = norm1_gain.reshape(1, model)
    gain2 = norm2_gain.reshape(1, model)
    block = spec((BLK, width))
    w_out_other = lax.ppermute(w_out, "mp", [(0, 1), (1, 0)])
    slots = store_map.T
    stay = lambda x: pltpu.with_memory_space_constraint(x, pltpu.HBM)

    near, across, far, stored = pl.pallas_call(
        pack_kernel,
        name="pack",
        out_shape=(block, block, block, spec((ROWS, width))),
        in_specs=[HBM, HBM, HBM],
        out_specs=(HBM,) * 4,
        scratch_shapes=[
            pltpu.SMEM(slots.shape, jnp.int32),
            pltpu.VMEM(bottleneck.shape, BF16),
            pltpu.VMEM((PAD, width), BF16),
            DMA((2 * STORE_DEV + 3,)),
        ],
        compiler_params=pltpu.CompilerParams(vmem_limit_bytes=4 << 20),
    )(stay(slots), stay(tokens), stay(bottleneck))
    across = partner(across, 3)
    near = partner(near, 1)
    far = partner(far, 2)
    stored_all = lax.all_gather(stored, "mp", axis=0)
    arrived = lax.all_gather(jnp.concatenate([near, across, far], axis=0), "mp", axis=0)

    near, across, far, own = pl.pallas_call(
        attend_kernel,
        name="attend",
        out_shape=(block, block, block, spec((BLK + PAD, width))),
        in_specs=[HBM, HBM, HBM, VMEM, VMEM, HBM, HBM],
        out_specs=(VMEM,) * 4,
        scratch_shapes=[
            pltpu.VMEM((CLIP_ROWS + PAD, model), BF16),
            pltpu.VMEM((CLIP_ROWS + 2 * BLK, heads_width), BF16),
            pltpu.VMEM((CLIP_ROWS + 2 * BLK, heads_width), BF16),
            pltpu.VMEM((CLIP_ROWS + 2 * BLK, heads_width), BF16),
            pltpu.VMEM((GROUP, BLK, heads_width), BF16),
            pltpu.VMEM(w_qkv.shape, BF16),
            pltpu.VMEM((1, model), F32),
            pltpu.SMEM(slots.shape, jnp.int32),
            pltpu.SMEM(clip_lengths.shape, jnp.int32),
            pltpu.SMEM(video_blocks.shape, jnp.int32),
            DMA((7,)),
        ],
        compiler_params=pltpu.CompilerParams(vmem_limit_bytes=24 << 20),
        cost_estimate=pl.CostEstimate(flops=2500000000, bytes_accessed=6000000, transcendentals=3000000),
    )(
        stay(slots),
        stay(clip_lengths),
        stay(video_blocks),
        stored_all,
        arrived,
        stay(gain1),
        stay(w_qkv),
    )
    across = partner(across, 3)
    near = partner(near, 1)
    far = partner(far, 2)
    own_all = lax.all_gather(own, "mp", axis=0)
    arrived = lax.all_gather(jnp.concatenate([near, across, far], axis=0), "mp", axis=0)

    base, send = pl.pallas_call(
        feed_kernel,
        name="feed",
        out_shape=(spec((ROWS, width), F32), spec((ROWS, width))),
        in_specs=[SMEM, VMEM, VMEM, VMEM, HBM, HBM, VMEM, HBM, HBM],
        out_specs=(VMEM,) * 2,
        scratch_shapes=[
            pltpu.VMEM((2, ROWS, width), BF16),
            pltpu.VMEM((ROWS, model), BF16),
            pltpu.VMEM((ROWS, model), BF16),
            pltpu.VMEM((ROWS, hidden), BF16),
            pltpu.VMEM((2, *w_out.shape), BF16),
            pltpu.VMEM(w_up.shape, BF16),
            pltpu.VMEM((2, hidden, width), BF16),
            DMA((2 + hidden // 512 + 2,)),
        ],
        compiler_params=pltpu.CompilerParams(vmem_limit_bytes=32 << 20),
        cost_estimate=pl.CostEstimate(flops=4100000000, bytes_accessed=14000000, transcendentals=820000),
    )(slots, stored_all, own_all, arrived, w_out, w_out_other, gain2, w_up, w_down)
    sums = lax.all_gather(send, "mp", axis=0)

    mixed, merged = pl.pallas_call(
        finish_kernel,
        name="finish",
        out_shape=(spec(tokens.shape), spec(bottleneck.shape)),
        in_specs=[SMEM, VMEM, VMEM],
        out_specs=(VMEM,) * 2,
        compiler_params=pltpu.CompilerParams(vmem_limit_bytes=8 << 20),
    )(slots, base, sums)
    return mixed, merged


def solution(mesh):
    placed = (
        P("clip", None, "mp"),
        P("clip", None, "mp"),
        P(),
        P(),
        P(),
        P(),
        P(None, None, "mp"),
        P("mp", None),
        P(),
        P(None, "mp"),
        P("mp", None),
    )
    return jax.shard_map(
        body,
        mesh=mesh,
        in_specs=placed,
        out_specs=(P("clip", None, "mp"), P("clip", None, "mp")),
        check_vma=False,
    )
```

time: 78.7 us -> 52.3 us (0.66)
  between operations: 14.1 us -> 0.71 us
  local copies, waits for them, and re-layouts: 11.3 us -> 0.02 us
  blocking collectives: 18 us -> 15.6 us
  starting transfers between devices: 10.6 us -> 12.8 us
  waiting for transfers between devices: 4.57 us -> 3.15 us
    unnamed x23 -> x10, local copies, waits for them, and re-layouts: 11.3 us -> 0.02 us
    ppermute x0 -> x1, starting transfers between devices: none -> 2.84 us  [body(): w_out_other = lax.ppermute(w_out, 'mp', [(0, 1), (1, 0)])]
    all_gather x1, blocking collectives: 5.06 us -> 2.87 us  [body(): stored_all = lax.all_gather(stored, 'mp', axis=0)]
    pallas_call x1, Pallas kernels: 6.77 us -> 8.46 us  [body(): pl.pallas_call(feed_kernel, name='feed', out_shape=(spec((ROWS, width), F...]
    pallas_call x1, Pallas kernels: 2.59 us -> 1.41 us  [body(): pl.pallas_call(finish_kernel, name='finish', out_shape=(spec(tokens.shape...]
  transfers between devices with their start and end apart: 7 -> 7, of which waited for: 2 -> 1; matrix products, arithmetic and copies ran while one was open for 2% -> 0% of each run, Pallas kernels for 13% -> 14%
where the time goes in v1:
time: 52.3 us; the launch traced here: 51.3 us
  Pallas kernels  18.9 us (36%)
  blocking collectives  15.6 us (30%)
  starting transfers between devices  12.8 us (24%)
  waiting for transfers between devices  3.15 us (6%)
  between operations  0.71 us (1%)
    ppermute x6, starting transfers between devices, partner(): lax.ppermute(x, 'clip', [(i, i ^ step) for i in range(lax.axis_size('clip...  9.99 us
    pallas_call x1, Pallas kernels, body(): pl.pallas_call(feed_kernel, name='feed', out_shape=(spec((ROWS, width), F...  8.46 us
    all_gather x2, blocking collectives, body(): lax.all_gather(jnp.concatenate([near, across, far], axis=0), 'mp', axis=0)  7.8 us
    pallas_call x1, Pallas kernels, body(): pl.pallas_call(attend_kernel, name='attend', out_shape=(block, block, blo...  7.03 us
    ppermute x6, waiting for transfers between devices, partner(): lax.ppermute(x, 'clip', [(i, i ^ step) for i in range(lax.axis_size('clip...  3.15 us
    all_gather x1, blocking collectives, body(): stored_all = lax.all_gather(stored, 'mp', axis=0)  2.87 us
    ppermute x1, starting transfers between devices, body(): w_out_other = lax.ppermute(w_out, 'mp', [(0, 1), (1, 0)])  2.84 us
    all_gather x1, blocking collectives, body(): own_all = lax.all_gather(own, 'mp', axis=0)  2.57 us
  transfers between devices with their start and end apart: 7, of which 1 were waited for; matrix products, arithmetic and copies ran while one was open for 0% of the time, Pallas kernels for 14%

profile of v1, /device:TPU:1, one launch (start us, length us, event | category | flops | bytes accessed | tf_op | source)
XLA Modules:
  0.0 51.3 jit_solution(10196730340251957106)
XLA Ops:
  0.6 2.0 %pack.1 = (bf16[128,512]{1,0:T(8,128)(2,1)S(1)}, bf16[128,512]{1,0:T(8,128)(2,1)S(1)}, bf16[128,512]{1,0:T(8,128)(2,1)S(1)}, bf16[400,512]{1,0:T(8,128)(2,1)S(1)}) custom-call(s32[3,128]{1,0:T(4,128)} %bitcast.14, bf16[3,128,512]{2,1,0:T(8,128)(2,1)} %tokens.1, bf16[1,4,512]{2,1,0:T(4,128)(2,1)} %extra.1), custom_call_target="tpu_custom_call" | custom-call | tf_op jit(solution)/shard_map/pack/pallas_call | solution.py:391
  2.6 2.1 %collective-permute-start = (bf16[128,512]{1,0:T(8,128)(2,1)S(1)}, bf16[128,512]{1,0:T(8,128)(2,1)S(1)}, u32[]{:S(2)}, u32[]{:S(2)}) collective-permute-start(bf16[128,512]{1,0:T(8,128)(2,1)S(1)} %get-tuple-element.13), channel_id=1, source_target_pairs={{0,2},{2,0},{4,6},{6,4},{8,10},{10,8},{12,14},{14,12},{16,18},{18,... | collective-permute-start | bytes 393224 | tf_op jit(solution)/shard_map/ppermute | solution.py:32
  4.7 1.8 %collective-permute-start.1 = (bf16[128,512]{1,0:T(8,128)(2,1)S(1)}, bf16[128,512]{1,0:T(8,128)(2,1)S(1)}, u32[]{:S(2)}, u32[]{:S(2)}) collective-permute-start(bf16[128,512]{1,0:T(8,128)(2,1)S(1)} %get-tuple-element.14), channel_id=1, source_target_pairs={{0,6},{2,4},{4,2},{6,0},{8,14},{10,12},{12,10},{14,8},{16,22},{18,... | collective-permute-start | bytes 393224 | tf_op jit(solution)/shard_map/ppermute | solution.py:32
  6.6 0.6 %collective-permute-start.2 = (bf16[128,512]{1,0:T(8,128)(2,1)S(1)}, bf16[128,512]{1,0:T(8,128)(2,1)S(1)}, u32[]{:S(2)}, u32[]{:S(2)}) collective-permute-start(bf16[128,512]{1,0:T(8,128)(2,1)S(1)} %get-tuple-element.15), channel_id=1, source_target_pairs={{0,4},{2,6},{4,0},{6,2},{8,12},{10,14},{12,8},{14,10},{16,20},{18,... | collective-permute-start | bytes 393224 | tf_op jit(solution)/shard_map/ppermute | solution.py:32
  7.2 2.8 %collective-permute-start.6 = (bf16[512,1024]{1,0:T(8,128)(2,1)}, bf16[512,1024]{1,0:T(8,128)(2,1)S(1)}, u32[]{:S(2)}, u32[]{:S(2)}) collective-permute-start(bf16[512,1024]{1,0:T(8,128)(2,1)} %w_out.1), channel_id=1, source_target_pairs={{0,1},{1,0},{2,3},{3,2},{4,5},{5,4},{6,7},{7,6},{8,9},{9,8},{10,11... | collective-permute-start | bytes 3145736 | tf_op jit(solution)/shard_map/ppermute | solution.py:387
  10.0 2.9 %all-gather = bf16[800,512]{1,0:T(8,128)(2,1)S(1)} all-gather(bf16[400,512]{1,0:T(8,128)(2,1)S(1)} %get-tuple-element.12), channel_id=2, replica_groups=mesh['clip'=128,'mp'=2] {'mp'}, dimensions={0}, use_global_device_ids=true | all-gather | bytes 1228800 | tf_op jit(solution)/shard_map/all_gather | solution.py:408
  12.9 0.0 collective-permute-done
  12.9 0.0 collective-permute-done.1
  12.9 0.0 collective-permute-done.2
  13.0 4.1 %all-gather.1 = bf16[768,512]{1,0:T(8,128)(2,1)S(1)} all-gather(bf16[384,512]{1,0:T(8,128)(2,1)S(1)} %pad_maximum_fusion), channel_id=3, replica_groups=mesh['clip'=128,'mp'=2] {'mp'}, dimensions={0}, use_global_device_ids=true | all-gather | bytes 1179648 | tf_op jit(solution)/shard_map/all_gather | solution.py:409
  17.1 0.0 copy-start
  17.1 0.0 copy-start.1
  17.1 0.0 copy-start.2
  17.1 0.0 copy-start.3
  17.1 0.0 copy-start.4
  17.1 7.0 %attend.1 = (bf16[128,512]{1,0:T(8,128)(2,1)S(1)}, bf16[128,512]{1,0:T(8,128)(2,1)S(1)}, bf16[128,512]{1,0:T(8,128)(2,1)S(1)}, bf16[144,512]{1,0:T(8,128)(2,1)S(1)}) custom-call(s32[3,128]{1,0:T(4,128)} %bitcast.15, s32[128]{0:T(128)} %all_lengths.1, s32[128]{0:T(128)} %all_videos.1, bf16[2,400,512]{2,1,0:T(8,128)(2,1)S(1)} %bitcast.9, ...), custom_call_target="tpu_custom_call" | custom-call | flops 2500000000 | bytes 6000000 | tf_op jit(solution)/shard_map/attend/pallas_call | solution.py:411
  24.1 0.5 %collective-permute-start.3 = (bf16[128,512]{1,0:T(8,128)(2,1)S(1)}, bf16[128,512]{1,0:T(8,128)(2,1)S(1)}, u32[]{:S(2)}, u32[]{:S(2)}) collective-permute-start(bf16[128,512]{1,0:T(8,128)(2,1)S(1)} %get-tuple-element.17), channel_id=1, source_target_pairs={{0,2},{2,0},{4,6},{6,4},{8,10},{10,8},{12,14},{14,12},{16,18},{18,... | collective-permute-start | bytes 393224 | tf_op jit(solution)/shard_map/ppermute | solution.py:32
  24.6 4.9 %collective-permute-start.4 = (bf16[128,512]{1,0:T(8,128)(2,1)S(1)}, bf16[128,512]{1,0:T(8,128)(2,1)S(1)}, u32[]{:S(2)}, u32[]{:S(2)}) collective-permute-start(bf16[128,512]{1,0:T(8,128)(2,1)S(1)} %get-tuple-element.18), channel_id=1, source_target_pairs={{0,6},{2,4},{4,2},{6,0},{8,14},{10,12},{12,10},{14,8},{16,22},{18,... | collective-permute-start | bytes 393224 | tf_op jit(solution)/shard_map/ppermute | solution.py:32
  29.5 0.0 collective-permute-start.5
  29.5 2.6 %all-gather.2 = bf16[288,512]{1,0:T(8,128)(2,1)S(1)} all-gather(bf16[144,512]{1,0:T(8,128)(2,1)S(1)} %get-tuple-element.16), channel_id=4, replica_groups=mesh['clip'=128,'mp'=2] {'mp'}, dimensions={0}, use_global_device_ids=true | all-gather | bytes 442368 | tf_op jit(solution)/shard_map/all_gather | solution.py:444
  32.1 0.0 collective-permute-done.3
  32.1 3.1 %collective-permute-done.4 = bf16[128,512]{1,0:T(8,128)(2,1)S(1)} collective-permute-done((bf16[128,512]{1,0:T(8,128)(2,1)S(1)}, bf16[128,512]{1,0:T(8,128)(2,1)S(1)}, u32[]{:S(2)}, u32[]{:S(2)}) %collective-permute-start.4) | collective-permute-done | bytes 131104 | tf_op jit(solution)/shard_map/ppermute | solution.py:32
  35.2 0.0 collective-permute-done.5
  35.3 3.7 %all-gather.3 = bf16[768,512]{1,0:T(8,128)(2,1)S(1)} all-gather(bf16[384,512]{1,0:T(8,128)(2,1)S(1)} %pad_maximum_fusion.1), channel_id=5, replica_groups=mesh['clip'=128,'mp'=2] {'mp'}, dimensions={0}, use_global_device_ids=true | all-gather | bytes 1179648 | tf_op jit(solution)/shard_map/all_gather | solution.py:445
  39.0 0.0 collective-permute-done.6.w_out_other
  39.0 0.0 copy-done
  39.0 0.0 copy-done.1
  39.0 0.0 copy-done.2
  39.0 0.0 copy-done.3
  39.0 0.0 copy-done.4
  39.0 8.5 %feed.1 = (f32[400,512]{1,0:T(8,128)S(1)}, bf16[400,512]{1,0:T(8,128)(2,1)S(1)}) custom-call(s32[3,128]{1,0:T(4,128)S(1)} %bitcast.16, bf16[2,400,512]{2,1,0:T(8,128)(2,1)S(1)} %bitcast.10, bf16[2,144,512]{2,1,0:T(8,128)(2,1)S(1)} %bitcast.13, bf16[2,384,512]{2,1,0:T(8,128)(2,1)S(1)} %bitcast.11, bf16[512,1024]{1,0:T(8,128)(2,1)S(1)} %copy-done.3, ...), custom_call_target="tpu_custom_call" | custom-call | flops 4100000000 | bytes 14000000 | tf_op jit(solution)/shard_map/feed/pallas_call | solution.py:447
  47.5 2.4 %all-gather.4 = bf16[800,512]{1,0:T(8,128)(2,1)S(1)} all-gather(bf16[400,512]{1,0:T(8,128)(2,1)S(1)} %get-tuple-element.21), channel_id=6, replica_groups=mesh['clip'=128,'mp'=2] {'mp'}, dimensions={0}, use_global_device_ids=true | all-gather | bytes 1228800 | tf_op jit(solution)/shard_map/all_gather | solution.py:466
  49.9 1.4 %finish.1 = (bf16[3,128,512]{2,1,0:T(8,128)(2,1)}, bf16[1,4,512]{2,1,0:T(4,128)(2,1)}) custom-call(s32[3,128]{1,0:T(4,128)S(1)} %bitcast.17, f32[400,512]{1,0:T(8,128)S(1)} %get-tuple-element.20.base, bf16[2,400,512]{2,1,0:T(8,128)(2,1)S(1)} %bitcast.8), custom_call_target="tpu_custom_call" | custom-call | tf_op jit(solution)/shard_map/finish/pallas_call | solution.py:468
  (2 shorter events, 0.1 us)
Async XLA Ops:
  2.6 10.3 %collective-permute-start = (bf16[128,512]{1,0:T(8,128)(2,1)S(1)}, bf16[128,512]{1,0:T(8,128)(2,1)S(1)}, u32[]{:S(2)}, u32[]{:S(2)}) collective-permute-start(bf16[128,512]{1,0:T(8,128)(2,1)S(1)} %get-tuple-element.13), channel_id=1, source_target_pairs={{0,2},{2,0},{4,6},{6,4},{8,10},{10,8},{12,14},{14,12},{16,18},{18,... | collective-permute-start | bytes 393224 | tf_op jit(solution)/shard_map/ppermute | solution.py:32
  4.7 8.2 %collective-permute-start.1 = (bf16[128,512]{1,0:T(8,128)(2,1)S(1)}, bf16[128,512]{1,0:T(8,128)(2,1)S(1)}, u32[]{:S(2)}, u32[]{:S(2)}) collective-permute-start(bf16[128,512]{1,0:T(8,128)(2,1)S(1)} %get-tuple-element.14), channel_id=1, source_target_pairs={{0,6},{2,4},{4,2},{6,0},{8,14},{10,12},{12,10},{14,8},{16,22},{18,... | collective-permute-start | bytes 393224 | tf_op jit(solution)/shard_map/ppermute | solution.py:32
  6.6 6.4 %collective-permute-start.2 = (bf16[128,512]{1,0:T(8,128)(2,1)S(1)}, bf16[128,512]{1,0:T(8,128)(2,1)S(1)}, u32[]{:S(2)}, u32[]{:S(2)}) collective-permute-start(bf16[128,512]{1,0:T(8,128)(2,1)S(1)} %get-tuple-element.15), channel_id=1, source_target_pairs={{0,4},{2,6},{4,0},{6,2},{8,12},{10,14},{12,8},{14,10},{16,20},{18,... | collective-permute-start | bytes 393224 | tf_op jit(solution)/shard_map/ppermute | solution.py:32
  7.2 31.8 %collective-permute-start.6 = (bf16[512,1024]{1,0:T(8,128)(2,1)}, bf16[512,1024]{1,0:T(8,128)(2,1)S(1)}, u32[]{:S(2)}, u32[]{:S(2)}) collective-permute-start(bf16[512,1024]{1,0:T(8,128)(2,1)} %w_out.1), channel_id=1, source_target_pairs={{0,1},{1,0},{2,3},{3,2},{4,5},{5,4},{6,7},{7,6},{8,9},{9,8},{10,11... | collective-permute-start | bytes 3145736 | tf_op jit(solution)/shard_map/ppermute | solution.py:387
  17.1 21.9 %copy-start = (s32[128,3]{0,1:T(4,128)S(1)}, s32[128,3]{0,1:T(4,128)}, u32[]{:S(2)}) copy-start(s32[128,3]{0,1:T(4,128)} %param.15) | copy-start | bytes 4612
  17.1 21.9 %copy-start.1 = (bf16[1024,2048]{1,0:T(8,128)(2,1)S(1)}, bf16[1024,2048]{1,0:T(8,128)(2,1)}, u32[]{:S(2)}) copy-start(bf16[1024,2048]{1,0:T(8,128)(2,1)} %w_up.1) | copy-start | bytes 12582916
  17.1 21.9 %copy-start.2 = (bf16[2048,1024]{1,0:T(8,128)(2,1)S(1)}, bf16[2048,1024]{1,0:T(8,128)(2,1)}, u32[]{:S(2)}) copy-start(bf16[2048,1024]{1,0:T(8,128)(2,1)} %w_down.1) | copy-start | bytes 12582916
  17.1 21.9 %copy-start.3 = (bf16[512,1024]{1,0:T(8,128)(2,1)S(1)}, bf16[512,1024]{1,0:T(8,128)(2,1)}, u32[]{:S(2)}) copy-start(bf16[512,1024]{1,0:T(8,128)(2,1)} %w_out.1) | copy-start | bytes 3145732
  17.1 21.9 %copy-start.4 = (f32[1024]{0:T(1024)S(1)}, f32[1024]{0:T(1024)}, u32[]{:S(2)}) copy-start(f32[1024]{0:T(1024)} %param.19) | copy-start | bytes 12292
  24.1 8.0 %collective-permute-start.3 = (bf16[128,512]{1,0:T(8,128)(2,1)S(1)}, bf16[128,512]{1,0:T(8,128)(2,1)S(1)}, u32[]{:S(2)}, u32[]{:S(2)}) collective-permute-start(bf16[128,512]{1,0:T(8,128)(2,1)S(1)} %get-tuple-element.17), channel_id=1, source_target_pairs={{0,2},{2,0},{4,6},{6,4},{8,10},{10,8},{12,14},{14,12},{16,18},{18,... | collective-permute-start | bytes 393224 | tf_op jit(solution)/shard_map/ppermute | solution.py:32
  24.6 10.6 %collective-permute-start.4 = (bf16[128,512]{1,0:T(8,128)(2,1)S(1)}, bf16[128,512]{1,0:T(8,128)(2,1)S(1)}, u32[]{:S(2)}, u32[]{:S(2)}) collective-permute-start(bf16[128,512]{1,0:T(8,128)(2,1)S(1)} %get-tuple-element.18), channel_id=1, source_target_pairs={{0,6},{2,4},{4,2},{6,0},{8,14},{10,12},{12,10},{14,8},{16,22},{18,... | collective-permute-start | bytes 393224 | tf_op jit(solution)/shard_map/ppermute | solution.py:32
  29.5 5.7 %collective-permute-start.5 = (bf16[128,512]{1,0:T(8,128)(2,1)S(1)}, bf16[128,512]{1,0:T(8,128)(2,1)S(1)}, u32[]{:S(2)}, u32[]{:S(2)}) collective-permute-start(bf16[128,512]{1,0:T(8,128)(2,1)S(1)} %get-tuple-element.19), channel_id=1, source_target_pairs={{0,4},{2,6},{4,0},{6,2},{8,12},{10,14},{12,8},{14,10},{16,20},{18,... | collective-permute-start | bytes 393224 | tf_op jit(solution)/shard_map/ppermute | solution.py:32

commit v2 on v1

v2 whole, which is shorter than its diff:
```python
import jax
import jax.numpy as jnp
from jax import lax
from jax.experimental import pallas as pl
from jax.experimental.pallas import tpu as pltpu
from jax.sharding import PartitionSpec as P

HEAD_DIM = 64
BLK = 128
NB = 4
SLOT_DEV = 4
STORE_DEV = 3
GROUP = 4
PAD = 16
STORED = STORE_DEV * BLK
ROWS = STORED + PAD
CLIP_ROWS = SLOT_DEV * BLK
BF16 = jnp.bfloat16
F32 = jnp.float32

VMEM = pl.BlockSpec(memory_space=pltpu.VMEM)
HBM = pl.BlockSpec(memory_space=pltpu.HBM)
DMA = pltpu.SemaphoreType.DMA
SMEM = pl.BlockSpec(memory_space=pltpu.SMEM)


def spec(shape, dtype=BF16):
    return jax.ShapeDtypeStruct(shape, dtype)


def partner(x, step):
    return lax.ppermute(x, "clip", [(i, i ^ step) for i in range(lax.axis_size("clip"))])


def slot_for(store_map, device, owner):
    slot = jnp.int32(-1)
    block = jnp.int32(-1)
    for s in range(STORE_DEV):
        entry = store_map[s, device]
        hit = (entry >= 0) & (entry // SLOT_DEV == owner)
        slot = jnp.where(hit, s, slot)
        block = jnp.where(hit, entry % SLOT_DEV, block)
    return slot, block


def norm_into(x0, x1, gain, out, at, rows):
    half = x0.shape[1]
    x0 = x0.astype(F32)
    x1 = x1.astype(F32)
    scale = 1.0 / (2 * half)
    mean = (jnp.sum(x0, axis=-1, keepdims=True) + jnp.sum(x1, axis=-1, keepdims=True)) * scale
    x0 = x0 - mean
    x1 = x1 - mean
    moment = (
        jnp.sum(x0 * x0, axis=-1, keepdims=True) + jnp.sum(x1 * x1, axis=-1, keepdims=True)
    ) * scale
    inv = lax.rsqrt(moment + 1e-05)
    out[pl.ds(at, rows), :half] = (x0 * inv * gain[:, :half]).astype(BF16)
    out[pl.ds(at, rows), half:] = (x1 * inv * gain[:, half:]).astype(BF16)


def pack_kernel(slots, tokens, extra, near, across, far, stored, store_map, few, tail, sems):
    member = lax.axis_index("clip")
    load_map = pltpu.make_async_copy(slots, store_map, sems.at[0])
    load_few = pltpu.make_async_copy(extra, few, sems.at[1])
    load_map.start()
    load_few.start()
    copies = [
        pltpu.make_async_copy(tokens.at[s], stored.at[pl.ds(s * BLK, BLK), :], sems.at[2 + s])
        for s in range(STORE_DEV)
    ]
    load_map.wait()
    for k, (step, out) in enumerate(((1, near), (3, across), (2, far))):
        slot, _ = slot_for(store_map, member, member ^ step)
        copies.append(
            pltpu.make_async_copy(tokens.at[jnp.maximum(slot, 0)], out, sems.at[2 + STORE_DEV + k])
        )
    for copy in copies:
        copy.start()
    load_few.wait()
    width = stored.shape[1]
    tail[...] = jnp.concatenate(
        [few[0].astype(F32), jnp.zeros((PAD - NB, width), F32)], axis=0
    ).astype(BF16)
    last = pltpu.make_async_copy(tail, stored.at[pl.ds(STORED, PAD), :], sems.at[2 + 2 * STORE_DEV])
    last.start()
    for copy in copies + [last]:
        copy.wait()


def attend_kernel(
    slots,
    all_lengths,
    all_videos,
    stored,
    arrived,
    gain_in,
    w_qkv,
    near,
    across,
    far,
    own,
    normed,
    query,
    keys,
    values,
    context,
    weights,
    info,
    gain,
    store_map,
    lengths,
    videos,
    sems,
):
    member = lax.axis_index("clip")
    small = [
        pltpu.make_async_copy(x, y, sems.at[i])
        for i, (x, y) in enumerate(
            ((gain_in, gain), (slots, store_map), (all_lengths, lengths), (all_videos, videos))
        )
    ]
    loads = [pltpu.make_async_copy(w_qkv.at[i], weights.at[i], sems.at[4 + i]) for i in range(3)]
    for load in small + loads:
        load.start()
    width = query.shape[1]
    for load in small:
        load.wait()
    gains = gain[...]
    for k in range(GROUP - 1):
        rows = slice(k * BLK, (k + 1) * BLK)
        norm_into(arrived[0, rows, :], arrived[1, rows, :], gains, normed, k * BLK, BLK)
    norm_into(stored[0, STORED:, :], stored[1, STORED:, :], gains, normed, CLIP_ROWS, PAD)

    length = lengths[member]
    video = videos[member]
    own_slot, own_block = slot_for(store_map, member, member)
    here = pl.multiple_of(jnp.maximum(own_slot, 0) * BLK, BLK)
    norm_into(
        stored[0, pl.ds(here, BLK), :],
        stored[1, pl.ds(here, BLK), :],
        gains,
        normed,
        (GROUP - 1) * BLK,
        BLK,
    )
    block_at = [slot_for(store_map, member ^ step, member)[1] for step in (1, 3, 2)] + [own_block]
    row_at = [
        pl.multiple_of(jnp.where(block < 0, SLOT_DEV + 1, block) * BLK, BLK) for block in block_at
    ]

    for place in range(GROUP):
        info[place] = block_at[place]

    tile = 256
    pairs = width // BLK
    end = CLIP_ROWS + PAD
    for which, out in ((0, query), (1, keys)):
        loads[which].wait()
        for j in range(0, width, tile):
            got = jnp.dot(normed[...], weights[which, :, j : j + tile], preferred_element_type=F32)
            if which == 0:
                got = got * HEAD_DIM ** (-0.5)
            got = got.astype(BF16)
            for place in range(GROUP):
                out[pl.ds(row_at[place], BLK), j : j + tile] = got[place * BLK : (place + 1) * BLK]
            out[CLIP_ROWS:end, j : j + tile] = got[CLIP_ROWS:]
    loads[2].wait()
    for p in range(pairs):
        if p % 2 == 0:
            j = p * BLK
            wide = jnp.dot(normed[...], weights[2, :, j : j + tile], preferred_element_type=F32)
        got = wide[:, p % 2 * BLK : (p % 2 + 1) * BLK]
        for place in range(GROUP):
            turned = got[place * BLK : (place + 1) * BLK].T
            values[p, :BLK, pl.ds(row_at[place], BLK)] = turned.astype(BF16)
        values[p, :BLK, CLIP_ROWS:end] = got[CLIP_ROWS:].T.astype(BF16)
        values[p, BLK:, :end] = jnp.ones((PAD, end), BF16)
    for b in range(2, SLOT_DEV):

        @pl.when(b >= length)
        def _():
            values[:, :BLK, b * BLK : (b + 1) * BLK] = jnp.zeros((pairs, BLK, BLK), BF16)

    context[...] = jnp.zeros_like(context)
    low = lax.broadcasted_iota(jnp.int32, (BLK, BLK), 1) < HEAD_DIM
    real = lax.broadcasted_iota(jnp.int32, (PAD, 2 * BLK), 0) < NB
    nt = (((1,), (1,)), ((), ()))

    def token_block(place, block, first, count):
        start = pl.multiple_of(first * BLK, BLK)
        at = pl.multiple_of(block * BLK, BLK)
        seen = count * BLK
        cols = [slice(p * BLK, (p + 1) * BLK) for p in range(pairs)]
        scores = []
        for p in range(pairs):
            q = query[pl.ds(at, BLK), cols[p]]
            none = jnp.zeros_like(q)
            both = jnp.concatenate([jnp.where(low, q, none), jnp.where(low, none, q)], axis=0)
            k = jnp.concatenate([keys[pl.ds(start, seen), cols[p]], keys[CLIP_ROWS:end, cols[p]]], axis=0)
            s = lax.dot_general(k, both, nt, preferred_element_type=F32)
            scores.append((s[:seen], jnp.where(real, s[seen:], -1e30)))
        tops = [
            jnp.maximum(jnp.max(s, axis=0, keepdims=True), jnp.max(se, axis=0, keepdims=True))
            for s, se in scores
        ]
        parts = [
            jnp.concatenate([jnp.exp(s - top).astype(BF16), jnp.exp(se - top).astype(BF16)], axis=0)
            for (s, se), top in zip(scores, tops)
        ]
        sums = []
        for p in range(pairs):
            v = jnp.concatenate([values[p, :, pl.ds(start, seen)], values[p, :, CLIP_ROWS:end]], axis=1)
            sums.append(jnp.dot(v, parts[p], preferred_element_type=F32))
        for p in range(pairs):
            o = sums[p]
            total = o[BLK : BLK + 1]
            o = jnp.concatenate(
                [o[:HEAD_DIM, :BLK] / total[:, :BLK], o[HEAD_DIM:BLK, BLK:] / total[:, BLK:]], axis=0
            )
            context[place, :, cols[p]] = o.T.astype(BF16)

    def visit(place, carry):
        block = info[place]
        is_video = block < video
        first = jnp.where(is_video, 0, video)
        seen = jnp.where(is_video, video, length - video)
        for count in range(1, SLOT_DEV):

            @pl.when((block >= 0) & (seen == count))
            def _():
                token_block(place, block, first, count)

        return carry

    lax.fori_loop(0, GROUP, visit, 0)

    heads = width // HEAD_DIM
    sub = 8
    qe = query[CLIP_ROWS:end, :].astype(F32)[:sub]
    qe = jnp.concatenate([qe] * heads, axis=0)
    row_head = lax.broadcasted_iota(jnp.int32, (heads * sub, width), 0) // sub
    col_head = lax.broadcasted_iota(jnp.int32, (heads * sub, width), 1) // HEAD_DIM
    qe = jnp.where(row_head == col_head, qe, 0.0).astype(BF16)
    s = lax.dot_general(qe, keys[:end, :], nt, preferred_element_type=F32)
    col = lax.broadcasted_iota(jnp.int32, s.shape, 1)
    bottle = (col >= CLIP_ROWS) & (col < CLIP_ROWS + NB)
    parts = []
    for allowed in (
        bottle | (col < video * BLK),
        bottle | ((col >= video * BLK) & (col < length * BLK)),
    ):
        masked = jnp.where(allowed, s, -1e30)
        e = jnp.exp(masked - jnp.max(masked, axis=-1, keepdims=True))
        parts.append((e / jnp.sum(e, axis=-1, keepdims=True)).astype(BF16))
    first_head = lax.broadcasted_iota(jnp.int32, (sub, BLK), 1) < HEAD_DIM
    for p in range(pairs):
        rows = slice(2 * p * sub, (2 * p + 2) * sub)
        both = jnp.concatenate([parts[0][rows], parts[1][rows]], axis=0)
        o = lax.dot_general(both, values[p, :BLK, :end], nt, preferred_element_type=F32)
        o = 0.5 * (o[: 2 * sub] + o[2 * sub :])
        o = jnp.where(first_head, o[:sub], o[sub:])
        own[BLK:, p * BLK : (p + 1) * BLK] = jnp.concatenate([o, jnp.zeros_like(o)], axis=0).astype(BF16)
    near[...] = context[0]
    across[...] = context[1]
    far[...] = context[2]
    own[:BLK, :] = context[3]


def feed_kernel(
    store_map,
    stored,
    own,
    arrived,
    w_out,
    w_out_other,
    gain,
    w_up,
    w_down,
    base,
    send,
    context,
    after,
    normed,
    active,
):
    member = lax.axis_index("clip")
    core = lax.axis_index("mp")
    half = base.shape[1]
    hidden = w_up.shape[1]
    sides = (core, 1 - core)
    for s in range(STORE_DEV):
        entry = store_map[s, member]
        step = jnp.where(entry >= 0, (entry // SLOT_DEV) ^ member, -1)
        at = jnp.where(step == 1, 0, jnp.where(step == 3, 1, 2))
        at = pl.multiple_of(at * BLK, BLK)
        rows = slice(s * BLK, (s + 1) * BLK)

        @pl.when(step == 0)
        def _():
            for k in range(2):
                context[k, rows, :] = own[sides[k], :BLK, :]

        @pl.when(step > 0)
        def _():
            for k in range(2):
                context[k, rows, :] = arrived[sides[k], pl.ds(at, BLK), :]

        @pl.when(step < 0)
        def _():
            for k in range(2):
                context[k, rows, :] = jnp.zeros((BLK, half), BF16)

    for k in range(2):
        context[k, STORED:, :] = own[sides[k], BLK:, :]

    tile = 256
    for j in range(0, 2 * half, tile):
        got = jnp.dot(context[0], w_out[:, j : j + tile], preferred_element_type=F32)
        got = got + jnp.dot(context[1], w_out_other[:, j : j + tile], preferred_element_type=F32)
        side, off = divmod(j, half)
        got = got + stored[side, :, off : off + tile].astype(F32)
        after[:, j : j + tile] = got.astype(BF16)
    gains = gain[...]
    for r in range(0, ROWS, 80):
        norm_into(after[r : r + 80, :half], after[r : r + 80, half:], gains, normed, r, 80)
    for j in range(0, hidden, tile):
        got = jnp.dot(normed[...], w_up[:, j : j + tile], preferred_element_type=F32)
        active[:, j : j + tile] = jax.nn.gelu(got, approximate=True).astype(BF16)
    for j in range(0, half, tile):
        other = pl.multiple_of((1 - core) * half + j, tile)
        got = jnp.dot(active[...], w_down[:, pl.ds(other, tile)], preferred_element_type=F32)
        send[:, j : j + tile] = got.astype(BF16)
        mine = pl.multiple_of(core * half + j, tile)
        got = jnp.dot(active[...], w_down[:, pl.ds(mine, tile)], preferred_element_type=F32)
        base[:, j : j + tile] = got + after[:, pl.ds(mine, tile)].astype(F32)


def finish_kernel(store_map, base, sums, mixed, merged):
    member = lax.axis_index("clip")
    core = lax.axis_index("mp")
    other = 1 - core
    for s in range(STORE_DEV):
        rows = slice(s * BLK, (s + 1) * BLK)
        got = base[rows, :] + sums[other, rows, :].astype(F32)
        keep = store_map[s, member] >= 0
        mixed[s] = jnp.where(keep, got, 0.0).astype(BF16)
    got = base[STORED:, :] + sums[other, STORED:, :].astype(F32)
    merged[0] = got[:NB].astype(BF16)


def stay(x):
    return pltpu.with_memory_space_constraint(x, pltpu.HBM)


def attend(slots, clip_lengths, video_blocks, stored_all, arrived, gain1, w_qkv):
    width = stored_all.shape[2]
    model = 2 * width
    heads_width = w_qkv.shape[2]
    block = spec((BLK, width))
    return pl.pallas_call(
        attend_kernel,
        name="attend",
        out_shape=(block, block, block, spec((BLK + PAD, width))),
        in_specs=[HBM, HBM, HBM, VMEM, VMEM, HBM, HBM],
        out_specs=(VMEM,) * 4,
        scratch_shapes=[
            pltpu.VMEM((CLIP_ROWS + PAD, model), BF16),
            pltpu.VMEM((CLIP_ROWS + 2 * BLK, heads_width), BF16),
            pltpu.VMEM((CLIP_ROWS + 2 * BLK, heads_width), BF16),
            pltpu.VMEM((heads_width // BLK, BLK + PAD, CLIP_ROWS + 2 * BLK), BF16),
            pltpu.VMEM((GROUP, BLK, heads_width), BF16),
            pltpu.VMEM(w_qkv.shape, BF16),
            pltpu.SMEM((GROUP,), jnp.int32),
            pltpu.VMEM((1, model), F32),
            pltpu.SMEM(slots.shape, jnp.int32),
            pltpu.SMEM(clip_lengths.shape, jnp.int32),
            pltpu.SMEM(video_blocks.shape, jnp.int32),
            DMA((7,)),
        ],
        compiler_params=pltpu.CompilerParams(vmem_limit_bytes=24 << 20),
        cost_estimate=pl.CostEstimate(flops=2500000000, bytes_accessed=6000000, transcendentals=3000000),
    )(
        stay(slots),
        stay(clip_lengths),
        stay(video_blocks),
        stored_all,
        arrived,
        stay(gain1),
        stay(w_qkv),
    )


def feed(slots, stored_all, own_all, arrived, w_out, w_out_other, gain2, w_up, w_down):
    width = stored_all.shape[2]
    model = 2 * width
    hidden = w_up.shape[1]
    return pl.pallas_call(
        feed_kernel,
        name="feed",
        out_shape=(spec((ROWS, width), F32), spec((ROWS, width))),
        in_specs=[SMEM] + [VMEM] * 8,
        out_specs=(VMEM,) * 2,
        scratch_shapes=[
            pltpu.VMEM((2, ROWS, width), BF16),
            pltpu.VMEM((ROWS, model), BF16),
            pltpu.VMEM((ROWS, model), BF16),
            pltpu.VMEM((ROWS, hidden), BF16),
        ],
        compiler_params=pltpu.CompilerParams(vmem_limit_bytes=16 << 20),
        cost_estimate=pl.CostEstimate(flops=4100000000, bytes_accessed=14000000, transcendentals=820000),
    )(slots, stored_all, own_all, arrived, w_out, w_out_other, gain2, w_up, w_down)


def body(
    tokens,
    bottleneck,
    clip_lengths,
    video_blocks,
    store_map,
    norm1_gain,
    w_qkv,
    w_out,
    norm2_gain,
    w_up,
    w_down,
):
    width = tokens.shape[2]
    model = 2 * width
    gain1 = norm1_gain.reshape(1, model)
    gain2 = norm2_gain.reshape(1, model)
    block = spec((BLK, width))
    w_out_other = lax.ppermute(w_out, "mp", [(0, 1), (1, 0)])
    slots = store_map.T

    near, across, far, stored = pl.pallas_call(
        pack_kernel,
        name="pack",
        out_shape=(block, block, block, spec((ROWS, width))),
        in_specs=[HBM, HBM, HBM],
        out_specs=(HBM,) * 4,
        scratch_shapes=[
            pltpu.SMEM(slots.shape, jnp.int32),
            pltpu.VMEM(bottleneck.shape, BF16),
            pltpu.VMEM((PAD, width), BF16),
            DMA((2 * STORE_DEV + 3,)),
        ],
        compiler_params=pltpu.CompilerParams(vmem_limit_bytes=4 << 20),
    )(stay(slots), stay(tokens), stay(bottleneck))
    across = partner(across, 3)
    near = partner(near, 1)
    far = partner(far, 2)
    stored_all = lax.all_gather(stored, "mp", axis=0)
    arrived = lax.all_gather(jnp.concatenate([near, across, far], axis=0), "mp", axis=0)

    near, across, far, own = attend(
        slots, clip_lengths, video_blocks, stored_all, arrived, gain1, w_qkv
    )
    across = partner(across, 3)
    near = partner(near, 1)
    far = partner(far, 2)
    own_all = lax.all_gather(own, "mp", axis=0)
    arrived = lax.all_gather(jnp.concatenate([near, across, far], axis=0), "mp", axis=0)

    base, send = feed(
        slots, stored_all, own_all, arrived, w_out, w_out_other, gain2, w_up, w_down
    )
    sums = lax.all_gather(send, "mp", axis=0)

    mixed, merged = pl.pallas_call(
        finish_kernel,
        name="finish",
        out_shape=(spec(tokens.shape), spec(bottleneck.shape)),
        in_specs=[SMEM, VMEM, VMEM],
        out_specs=(VMEM,) * 2,
        compiler_params=pltpu.CompilerParams(vmem_limit_bytes=8 << 20),
    )(slots, base, sums)
    return mixed, merged


def solution(mesh):
    placed = (
        P("clip", None, "mp"),
        P("clip", None, "mp"),
        P(),
        P(),
        P(),
        P(),
        P(None, None, "mp"),
        P("mp", None),
        P(),
        P(None, "mp"),
        P("mp", None),
    )
    return jax.shard_map(
        body,
        mesh=mesh,
        in_specs=placed,
        out_specs=(P("clip", None, "mp"), P("clip", None, "mp")),
        check_vma=False,
    )
```

time: 52.3 us -> 47.5 us (0.908); the launches traced: 51.3 us -> 47.9 us
  starting transfers between devices: 12.8 us -> 10.8 us
  Pallas kernels: 18.9 us -> 17.6 us
  blocking collectives: 15.6 us -> 15 us
    ppermute x6, starting transfers between devices: 9.99 us -> 7.92 us  [partner(): lax.ppermute(x, 'clip', [(i, i ^ step) for i in range(lax.axis_size('clip...]
    pallas_call x2, Pallas kernels: 15.5 us -> 14.2 us  [the longest x1 8.33 us: attend(): pl.pallas_call(attend_kernel, name='attend', out_shape=(block, block, blo...]
    all_gather x2, blocking collectives: 7.8 us -> 6.91 us  [body(): lax.all_gather(jnp.concatenate([near, across, far], axis=0), 'mp', axis=0)]
  transfers between devices with their start and end apart: 7 -> 7, of which waited for: 1 -> 1; matrix products, arithmetic and copies ran while one was open for 0% -> 0% of each run, Pallas kernels for 14% -> 17%
where the time goes in v2:
time: 47.5 us; the launch traced here: 47.9 us
  Pallas kernels  17.6 us (37%)
  blocking collectives  15 us (32%)
  starting transfers between devices  10.8 us (23%)
  waiting for transfers between devices  3.66 us (8%)
  between operations  0.71 us (1%)
    pallas_call x1, Pallas kernels, attend(): pl.pallas_call(attend_kernel, name='attend', out_shape=(block, block, blo...  8.33 us
    ppermute x6, starting transfers between devices, partner(): lax.ppermute(x, 'clip', [(i, i ^ step) for i in range(lax.axis_size('clip...  7.92 us
    all_gather x2, blocking collectives, body(): lax.all_gather(jnp.concatenate([near, across, far], axis=0), 'mp', axis=0)  6.91 us
    pallas_call x1, Pallas kernels, feed(): pl.pallas_call(feed_kernel, name='feed', out_shape=(spec((ROWS, width), F...  5.91 us
    ppermute x6, waiting for transfers between devices, partner(): lax.ppermute(x, 'clip', [(i, i ^ step) for i in range(lax.axis_size('clip...  3.66 us
    all_gather x1, blocking collectives, body(): stored_all = lax.all_gather(stored, 'mp', axis=0)  2.87 us
    all_gather x1, blocking collectives, body(): own_all = lax.all_gather(own, 'mp', axis=0)  2.86 us
    ppermute x1, starting transfers between devices, body(): w_out_other = lax.ppermute(w_out, 'mp', [(0, 1), (1, 0)])  2.84 us
  transfers between devices with their start and end apart: 7, of which 1 were waited for; matrix products, arithmetic and copies ran while one was open for 0% of the time, Pallas kernels for 17%

profile of v2, /device:TPU:1, one launch (start us, length us, event | category | flops | bytes accessed | tf_op | source)
XLA Modules:
  0.0 47.9 jit_solution(2031976807026797307)
XLA Ops:
  0.6 2.0 %pack.1 = (bf16[128,512]{1,0:T(8,128)(2,1)S(1)}, bf16[128,512]{1,0:T(8,128)(2,1)S(1)}, bf16[128,512]{1,0:T(8,128)(2,1)S(1)}, bf16[400,512]{1,0:T(8,128)(2,1)S(1)}) custom-call(s32[3,128]{1,0:T(4,128)} %bitcast.14, bf16[3,128,512]{2,1,0:T(8,128)(2,1)} %tokens.1, bf16[1,4,512]{2,1,0:T(4,128)(2,1)} %extra.1), custom_call_target="tpu_custom_call" | custom-call | tf_op jit(solution)/shard_map/pack/pallas_call | solution.py:436
  2.6 2.1 %collective-permute-start = (bf16[128,512]{1,0:T(8,128)(2,1)S(1)}, bf16[128,512]{1,0:T(8,128)(2,1)S(1)}, u32[]{:S(2)}, u32[]{:S(2)}) collective-permute-start(bf16[128,512]{1,0:T(8,128)(2,1)S(1)} %get-tuple-element.13), channel_id=1, source_target_pairs={{0,2},{2,0},{4,6},{6,4},{8,10},{10,8},{12,14},{14,12},{16,18},{18,... | collective-permute-start | bytes 393224 | tf_op jit(solution)/shard_map/ppermute | solution.py:32
  4.7 1.8 %collective-permute-start.1 = (bf16[128,512]{1,0:T(8,128)(2,1)S(1)}, bf16[128,512]{1,0:T(8,128)(2,1)S(1)}, u32[]{:S(2)}, u32[]{:S(2)}) collective-permute-start(bf16[128,512]{1,0:T(8,128)(2,1)S(1)} %get-tuple-element.14), channel_id=1, source_target_pairs={{0,6},{2,4},{4,2},{6,0},{8,14},{10,12},{12,10},{14,8},{16,22},{18,... | collective-permute-start | bytes 393224 | tf_op jit(solution)/shard_map/ppermute | solution.py:32
  6.6 0.6 %collective-permute-start.2 = (bf16[128,512]{1,0:T(8,128)(2,1)S(1)}, bf16[128,512]{1,0:T(8,128)(2,1)S(1)}, u32[]{:S(2)}, u32[]{:S(2)}) collective-permute-start(bf16[128,512]{1,0:T(8,128)(2,1)S(1)} %get-tuple-element.15), channel_id=1, source_target_pairs={{0,4},{2,6},{4,0},{6,2},{8,12},{10,14},{12,8},{14,10},{16,20},{18,... | collective-permute-start | bytes 393224 | tf_op jit(solution)/shard_map/ppermute | solution.py:32
  7.2 2.8 %collective-permute-start.6 = (bf16[512,1024]{1,0:T(8,128)(2,1)}, bf16[512,1024]{1,0:T(8,128)(2,1)S(1)}, u32[]{:S(2)}, u32[]{:S(2)}) collective-permute-start(bf16[512,1024]{1,0:T(8,128)(2,1)} %w_out.1), channel_id=1, source_target_pairs={{0,1},{1,0},{2,3},{3,2},{4,5},{5,4},{6,7},{7,6},{8,9},{9,8},{10,11... | collective-permute-start | bytes 3145736 | tf_op jit(solution)/shard_map/ppermute | solution.py:433
  10.0 2.9 %all-gather = bf16[800,512]{1,0:T(8,128)(2,1)S(1)} all-gather(bf16[400,512]{1,0:T(8,128)(2,1)S(1)} %get-tuple-element.12), channel_id=2, replica_groups=mesh['clip'=128,'mp'=2] {'mp'}, dimensions={0}, use_global_device_ids=true | all-gather | bytes 1228800 | tf_op jit(solution)/shard_map/all_gather | solution.py:453
  12.9 0.0 collective-permute-done
  12.9 0.0 collective-permute-done.1
  12.9 0.0 collective-permute-done.2
  13.0 4.1 %all-gather.1 = bf16[768,512]{1,0:T(8,128)(2,1)S(1)} all-gather(bf16[384,512]{1,0:T(8,128)(2,1)S(1)} %pad_maximum_fusion), channel_id=3, replica_groups=mesh['clip'=128,'mp'=2] {'mp'}, dimensions={0}, use_global_device_ids=true | all-gather | bytes 1179648 | tf_op jit(solution)/shard_map/all_gather | solution.py:454
  17.1 0.0 copy-start
  17.1 0.0 copy-start.1
  17.1 0.0 copy-start.2
  17.1 0.0 copy-start.3
  17.1 0.0 copy-start.4
  17.1 8.3 %attend.1 = (bf16[128,512]{1,0:T(8,128)(2,1)S(1)}, bf16[128,512]{1,0:T(8,128)(2,1)S(1)}, bf16[128,512]{1,0:T(8,128)(2,1)S(1)}, bf16[144,512]{1,0:T(8,128)(2,1)S(1)}) custom-call(s32[3,128]{1,0:T(4,128)} %bitcast.15, s32[128]{0:T(128)} %all_lengths.1, s32[128]{0:T(128)} %all_videos.1, bf16[2,400,512]{2,1,0:T(8,128)(2,1)S(1)} %bitcast.9, ...), custom_call_target="tpu_custom_call" | custom-call | flops 2500000000 | bytes 6000000 | tf_op jit(solution)/shard_map/attend/pallas_call | solution.py:361
  25.4 0.7 %collective-permute-start.3 = (bf16[128,512]{1,0:T(8,128)(2,1)S(1)}, bf16[128,512]{1,0:T(8,128)(2,1)S(1)}, u32[]{:S(2)}, u32[]{:S(2)}) collective-permute-start(bf16[128,512]{1,0:T(8,128)(2,1)S(1)} %get-tuple-element.17), channel_id=1, source_target_pairs={{0,2},{2,0},{4,6},{6,4},{8,10},{10,8},{12,14},{14,12},{16,18},{18,... | collective-permute-start | bytes 393224 | tf_op jit(solution)/shard_map/ppermute | solution.py:32
  26.1 0.0 collective-permute-start.4
  26.2 2.6 %collective-permute-start.5 = (bf16[128,512]{1,0:T(8,128)(2,1)S(1)}, bf16[128,512]{1,0:T(8,128)(2,1)S(1)}, u32[]{:S(2)}, u32[]{:S(2)}) collective-permute-start(bf16[128,512]{1,0:T(8,128)(2,1)S(1)} %get-tuple-element.19), channel_id=1, source_target_pairs={{0,4},{2,6},{4,0},{6,2},{8,12},{10,14},{12,8},{14,10},{16,20},{18,... | collective-permute-start | bytes 393224 | tf_op jit(solution)/shard_map/ppermute | solution.py:32
  28.8 2.9 %all-gather.2 = bf16[288,512]{1,0:T(8,128)(2,1)S(1)} all-gather(bf16[144,512]{1,0:T(8,128)(2,1)S(1)} %get-tuple-element.16), channel_id=4, replica_groups=mesh['clip'=128,'mp'=2] {'mp'}, dimensions={0}, use_global_device_ids=true | all-gather | bytes 442368 | tf_op jit(solution)/shard_map/all_gather | solution.py:462
  31.6 0.0 collective-permute-done.3
  31.6 3.6 %collective-permute-done.4 = bf16[128,512]{1,0:T(8,128)(2,1)S(1)} collective-permute-done((bf16[128,512]{1,0:T(8,128)(2,1)S(1)}, bf16[128,512]{1,0:T(8,128)(2,1)S(1)}, u32[]{:S(2)}, u32[]{:S(2)}) %collective-permute-start.4) | collective-permute-done | bytes 131104 | tf_op jit(solution)/shard_map/ppermute | solution.py:32
  35.3 0.0 collective-permute-done.5
  35.3 2.8 %all-gather.3 = bf16[768,512]{1,0:T(8,128)(2,1)S(1)} all-gather(bf16[384,512]{1,0:T(8,128)(2,1)S(1)} %pad_maximum_fusion.1), channel_id=5, replica_groups=mesh['clip'=128,'mp'=2] {'mp'}, dimensions={0}, use_global_device_ids=true | all-gather | bytes 1179648 | tf_op jit(solution)/shard_map/all_gather | solution.py:463
  38.1 0.0 collective-permute-done.6.w_out_other
  38.1 0.0 copy-done
  38.1 0.0 copy-done.1
  38.1 0.0 copy-done.2
  38.1 0.0 copy-done.3
  38.1 0.0 copy-done.4
  38.1 5.9 %feed.1 = (f32[400,512]{1,0:T(8,128)S(1)}, bf16[400,512]{1,0:T(8,128)(2,1)S(1)}) custom-call(s32[3,128]{1,0:T(4,128)S(1)} %bitcast.16, bf16[2,400,512]{2,1,0:T(8,128)(2,1)S(1)} %bitcast.10, bf16[2,144,512]{2,1,0:T(8,128)(2,1)S(1)} %bitcast.13, bf16[2,384,512]{2,1,0:T(8,128)(2,1)S(1)} %bitcast.11, bf16[512,1024]{1,0:T(8,128)(2,1)S(1)} %copy-done.3, ...), custom_call_target="tpu_custom_call" | custom-call | flops 4100000000 | bytes 14000000 | tf_op jit(solution)/shard_map/feed/pallas_call | solution.py:398
  44.1 2.4 %all-gather.4 = bf16[800,512]{1,0:T(8,128)(2,1)S(1)} all-gather(bf16[400,512]{1,0:T(8,128)(2,1)S(1)} %get-tuple-element.21), channel_id=6, replica_groups=mesh['clip'=128,'mp'=2] {'mp'}, dimensions={0}, use_global_device_ids=true | all-gather | bytes 1228800 | tf_op jit(solution)/shard_map/all_gather | solution.py:468
  46.5 1.4 %finish.1 = (bf16[3,128,512]{2,1,0:T(8,128)(2,1)}, bf16[1,4,512]{2,1,0:T(4,128)(2,1)}) custom-call(s32[3,128]{1,0:T(4,128)S(1)} %bitcast.17, f32[400,512]{1,0:T(8,128)S(1)} %get-tuple-element.20.base, bf16[2,400,512]{2,1,0:T(8,128)(2,1)S(1)} %bitcast.8), custom_call_target="tpu_custom_call" | custom-call | tf_op jit(solution)/shard_map/finish/pallas_call | solution.py:470
  (2 shorter events, 0.1 us)
Async XLA Ops:
  2.6 10.3 %collective-permute-start = (bf16[128,512]{1,0:T(8,128)(2,1)S(1)}, bf16[128,512]{1,0:T(8,128)(2,1)S(1)}, u32[]{:S(2)}, u32[]{:S(2)}) collective-permute-start(bf16[128,512]{1,0:T(8,128)(2,1)S(1)} %get-tuple-element.13), channel_id=1, source_target_pairs={{0,2},{2,0},{4,6},{6,4},{8,10},{10,8},{12,14},{14,12},{16,18},{18,... | collective-permute-start | bytes 393224 | tf_op jit(solution)/shard_map/ppermute | solution.py:32
  4.7 8.2 %collective-permute-start.1 = (bf16[128,512]{1,0:T(8,128)(2,1)S(1)}, bf16[128,512]{1,0:T(8,128)(2,1)S(1)}, u32[]{:S(2)}, u32[]{:S(2)}) collective-permute-start(bf16[128,512]{1,0:T(8,128)(2,1)S(1)} %get-tuple-element.14), channel_id=1, source_target_pairs={{0,6},{2,4},{4,2},{6,0},{8,14},{10,12},{12,10},{14,8},{16,22},{18,... | collective-permute-start | bytes 393224 | tf_op jit(solution)/shard_map/ppermute | solution.py:32
  6.6 6.4 %collective-permute-start.2 = (bf16[128,512]{1,0:T(8,128)(2,1)S(1)}, bf16[128,512]{1,0:T(8,128)(2,1)S(1)}, u32[]{:S(2)}, u32[]{:S(2)}) collective-permute-start(bf16[128,512]{1,0:T(8,128)(2,1)S(1)} %get-tuple-element.15), channel_id=1, source_target_pairs={{0,4},{2,6},{4,0},{6,2},{8,12},{10,14},{12,8},{14,10},{16,20},{18,... | collective-permute-start | bytes 393224 | tf_op jit(solution)/shard_map/ppermute | solution.py:32
  7.2 30.9 %collective-permute-start.6 = (bf16[512,1024]{1,0:T(8,128)(2,1)}, bf16[512,1024]{1,0:T(8,128)(2,1)S(1)}, u32[]{:S(2)}, u32[]{:S(2)}) collective-permute-start(bf16[512,1024]{1,0:T(8,128)(2,1)} %w_out.1), channel_id=1, source_target_pairs={{0,1},{1,0},{2,3},{3,2},{4,5},{5,4},{6,7},{7,6},{8,9},{9,8},{10,11... | collective-permute-start | bytes 3145736 | tf_op jit(solution)/shard_map/ppermute | solution.py:433
  17.1 21.1 %copy-start = (s32[128,3]{0,1:T(4,128)S(1)}, s32[128,3]{0,1:T(4,128)}, u32[]{:S(2)}) copy-start(s32[128,3]{0,1:T(4,128)} %param.15) | copy-start | bytes 4612
  17.1 21.1 %copy-start.1 = (bf16[1024,2048]{1,0:T(8,128)(2,1)S(1)}, bf16[1024,2048]{1,0:T(8,128)(2,1)}, u32[]{:S(2)}) copy-start(bf16[1024,2048]{1,0:T(8,128)(2,1)} %w_up.1) | copy-start | bytes 12582916
  17.1 21.1 %copy-start.2 = (bf16[2048,1024]{1,0:T(8,128)(2,1)S(1)}, bf16[2048,1024]{1,0:T(8,128)(2,1)}, u32[]{:S(2)}) copy-start(bf16[2048,1024]{1,0:T(8,128)(2,1)} %w_down.1) | copy-start | bytes 12582916
  17.1 21.1 %copy-start.3 = (bf16[512,1024]{1,0:T(8,128)(2,1)S(1)}, bf16[512,1024]{1,0:T(8,128)(2,1)}, u32[]{:S(2)}) copy-start(bf16[512,1024]{1,0:T(8,128)(2,1)} %w_out.1) | copy-start | bytes 3145732
  17.1 21.1 %copy-start.4 = (f32[1024]{0:T(1024)S(1)}, f32[1024]{0:T(1024)}, u32[]{:S(2)}) copy-start(f32[1024]{0:T(1024)} %param.19) | copy-start | bytes 12292
  25.4 6.2 %collective-permute-start.3 = (bf16[128,512]{1,0:T(8,128)(2,1)S(1)}, bf16[128,512]{1,0:T(8,128)(2,1)S(1)}, u32[]{:S(2)}, u32[]{:S(2)}) collective-permute-start(bf16[128,512]{1,0:T(8,128)(2,1)S(1)} %get-tuple-element.17), channel_id=1, source_target_pairs={{0,2},{2,0},{4,6},{6,4},{8,10},{10,8},{12,14},{14,12},{16,18},{18,... | collective-permute-start | bytes 393224 | tf_op jit(solution)/shard_map/ppermute | solution.py:32
  26.1 9.1 %collective-permute-start.4 = (bf16[128,512]{1,0:T(8,128)(2,1)S(1)}, bf16[128,512]{1,0:T(8,128)(2,1)S(1)}, u32[]{:S(2)}, u32[]{:S(2)}) collective-permute-start(bf16[128,512]{1,0:T(8,128)(2,1)S(1)} %get-tuple-element.18), channel_id=1, source_target_pairs={{0,6},{2,4},{4,2},{6,0},{8,14},{10,12},{12,10},{14,8},{16,22},{18,... | collective-permute-start | bytes 393224 | tf_op jit(solution)/shard_map/ppermute | solution.py:32
  26.2 9.1 %collective-permute-start.5 = (bf16[128,512]{1,0:T(8,128)(2,1)S(1)}, bf16[128,512]{1,0:T(8,128)(2,1)S(1)}, u32[]{:S(2)}, u32[]{:S(2)}) collective-permute-start(bf16[128,512]{1,0:T(8,128)(2,1)S(1)} %get-tuple-element.19), channel_id=1, source_target_pairs={{0,4},{2,6},{4,0},{6,2},{8,12},{10,14},{12,8},{14,10},{16,20},{18,... | collective-permute-start | bytes 393224 | tf_op jit(solution)/shard_map/ppermute | solution.py:32

commit v3 on v2

--- a/solution.py
+++ b/solution.py
@@ -88,24 +88,122 @@
         copy.wait()
 
 
+def ready_kernel(slots, gain_in, w_qkv, stored, weights, query, keys, values, normed, gain, store_map, sems):
+    member = lax.axis_index("clip")
+    small = [
+        pltpu.make_async_copy(x, y, sems.at[i])
+        for i, (x, y) in enumerate(((gain_in, gain), (slots, store_map)))
+    ]
+    loads = [pltpu.make_async_copy(w_qkv.at[i], weights.at[i], sems.at[2 + i]) for i in range(3)]
+    for load in small + loads:
+        load.start()
+    small[0].wait()
+    gains = gain[...]
+    norm_into(stored[0, STORED:, :], stored[1, STORED:, :], gains, normed, BLK, PAD)
+    small[1].wait()
+    slot, _ = slot_for(store_map, member, member)
+    here = pl.multiple_of(jnp.maximum(slot, 0) * BLK, BLK)
+    norm_into(
+        stored[0, pl.ds(here, BLK), :], stored[1, pl.ds(here, BLK), :], gains, normed, 0, BLK
+    )
+    width = query.shape[1]
+    tile = 256
+    for which, out in ((0, query), (1, keys)):
+        loads[which].wait()
+        for j in range(0, width, tile):
+            got = jnp.dot(normed[...], weights[which, :, j : j + tile], preferred_element_type=F32)
+            if which == 0:
+                got = got * HEAD_DIM ** (-0.5)
+            out[:, j : j + tile] = got.astype(BF16)
+    loads[2].wait()
+    for j in range(0, width, tile):
+        got = jnp.dot(normed[...], weights[2, :, j : j + tile], preferred_element_type=F32)
+        for k in range(tile // BLK):
+            p = j // BLK + k
+            cols = slice(k * BLK, (k + 1) * BLK)
+            values[p, :, :BLK] = got[:BLK, cols].T.astype(BF16)
+            values[p, :, BLK:] = got[BLK:, cols].T.astype(BF16)
+
+
+NT = (((1,), (1,)), ((), ()))
+END = CLIP_ROWS + PAD
+
+
+def token_block(query, keys, values, context, place, block, first, count):
+    pairs = values.shape[0]
+    low = lax.broadcasted_iota(jnp.int32, (BLK, BLK), 1) < HEAD_DIM
+    real = lax.broadcasted_iota(jnp.int32, (PAD, 2 * BLK), 0) < NB
+    start = pl.multiple_of(first * BLK, BLK)
+    at = pl.multiple_of(block * BLK, BLK)
+    seen = count * BLK
+    cols = [slice(p * BLK, (p + 1) * BLK) for p in range(pairs)]
+    scores = []
+    for p in range(pairs):
+        q = query[pl.ds(at, BLK), cols[p]]
+        none = jnp.zeros_like(q)
+        both = jnp.concatenate([jnp.where(low, q, none), jnp.where(low, none, q)], axis=0)
+        k = jnp.concatenate([keys[pl.ds(start, seen), cols[p]], keys[CLIP_ROWS:END, cols[p]]], axis=0)
+        s = lax.dot_general(k, both, NT, preferred_element_type=F32)
+        scores.append((s[:seen], jnp.where(real, s[seen:], -1e30)))
+    tops = [
+        jnp.maximum(jnp.max(s, axis=0, keepdims=True), jnp.max(se, axis=0, keepdims=True))
+        for s, se in scores
+    ]
+    parts = [
+        jnp.concatenate([jnp.exp(s - top).astype(BF16), jnp.exp(se - top).astype(BF16)], axis=0)
+        for (s, se), top in zip(scores, tops)
+    ]
+    sums = []
+    for p in range(pairs):
+        v = jnp.concatenate([values[p, :, pl.ds(start, seen)], values[p, :, CLIP_ROWS:END]], axis=1)
+        sums.append(jnp.dot(v, parts[p], preferred_element_type=F32))
+    for p in range(pairs):
+        o = sums[p]
+        total = o[BLK : BLK + 1]
+        o = jnp.concatenate(
+            [o[:HEAD_DIM, :BLK] / total[:, :BLK], o[HEAD_DIM:BLK, BLK:] / total[:, BLK:]], axis=0
+        )
+        context[place, :, cols[p]] = o.T.astype(BF16)
+
+
+def visit_blocks(info, places, query, keys, values, context):
+    def visit(i, carry):
+        place = places[0] + i * (places[1] - places[0])
+        block = info[0, place]
+        length = info[0, GROUP]
+        video = info[0, GROUP + 1]
+        is_video = block < video
+        first = jnp.where(is_video, 0, video)
+        seen = jnp.where(is_video, video, length - video)
+        for count in range(1, SLOT_DEV):
+
+            @pl.when((block >= 0) & (seen == count))
+            def _():
+                token_block(query, keys, values, context, i, block, first, count)
+
+        return carry
+
+    lax.fori_loop(0, 2, visit, 0)
+
+
 def attend_kernel(
     slots,
     all_lengths,
     all_videos,
-    stored,
+    gain_in,
     arrived,
-    gain_in,
-    w_qkv,
-    near,
+    weights,
+    own_query,
+    own_keys,
+    own_values,
     across,
     far,
-    own,
-    normed,
     query,
     keys,
     values,
+    facts,
+    normed,
     context,
-    weights,
     info,
     gain,
     store_map,
@@ -120,129 +218,89 @@
             ((gain_in, gain), (slots, store_map), (all_lengths, lengths), (all_videos, videos))
         )
     ]
-    loads = [pltpu.make_async_copy(w_qkv.at[i], weights.at[i], sems.at[4 + i]) for i in range(3)]
-    for load in small + loads:
+    for load in small:
         load.start()
     width = query.shape[1]
-    for load in small:
-        load.wait()
+    pairs = width // BLK
+    context[...] = jnp.zeros_like(context)
+    small[0].wait()
     gains = gain[...]
     for k in range(GROUP - 1):
         rows = slice(k * BLK, (k + 1) * BLK)
         norm_into(arrived[0, rows, :], arrived[1, rows, :], gains, normed, k * BLK, BLK)
-    norm_into(stored[0, STORED:, :], stored[1, STORED:, :], gains, normed, CLIP_ROWS, PAD)
-
+    for load in small[1:]:
+        load.wait()
     length = lengths[member]
     video = videos[member]
-    own_slot, own_block = slot_for(store_map, member, member)
-    here = pl.multiple_of(jnp.maximum(own_slot, 0) * BLK, BLK)
-    norm_into(
-        stored[0, pl.ds(here, BLK), :],
-        stored[1, pl.ds(here, BLK), :],
-        gains,
-        normed,
-        (GROUP - 1) * BLK,
-        BLK,
-    )
-    block_at = [slot_for(store_map, member ^ step, member)[1] for step in (1, 3, 2)] + [own_block]
+    block_at = [slot_for(store_map, member ^ step, member)[1] for step in (1, 3, 2, 0)]
     row_at = [
         pl.multiple_of(jnp.where(block < 0, SLOT_DEV + 1, block) * BLK, BLK) for block in block_at
     ]
-
     for place in range(GROUP):
-        info[place] = block_at[place]
-
+        info[0, place] = block_at[place]
+    info[0, GROUP] = length
+    info[0, GROUP + 1] = video
+    keep = pltpu.make_async_copy(info, facts, sems.at[4])
+    keep.start()
+
+    last = GROUP - 1
+    for own, out in ((own_query, query), (own_keys, keys)):
+        out[pl.ds(row_at[last], BLK), :] = own[:BLK, :]
+        out[CLIP_ROWS:END, :] = own[BLK:, :]
+    for p in range(pairs):
+        values[p, :BLK, pl.ds(row_at[last], BLK)] = own_values[p, :, :BLK]
+        values[p, :BLK, CLIP_ROWS:END] = own_values[p, :, BLK:]
+        values[p, BLK:, :END] = jnp.ones((PAD, END), BF16)
     tile = 256
-    pairs = width // BLK
-    end = CLIP_ROWS + PAD
     for which, out in ((0, query), (1, keys)):
-        loads[which].wait()
         for j in range(0, width, tile):
             got = jnp.dot(normed[...], weights[which, :, j : j + tile], preferred_element_type=F32)
             if which == 0:
                 got = got * HEAD_DIM ** (-0.5)
             got = got.astype(BF16)
-            for place in range(GROUP):
+            for place in range(last):
                 out[pl.ds(row_at[place], BLK), j : j + tile] = got[place * BLK : (place + 1) * BLK]
-            out[CLIP_ROWS:end, j : j + tile] = got[CLIP_ROWS:]
-    loads[2].wait()
-    for p in range(pairs):
-        if p % 2 == 0:
-            j = p * BLK
-            wide = jnp.dot(normed[...], weights[2, :, j : j + tile], preferred_element_type=F32)
-        got = wide[:, p % 2 * BLK : (p % 2 + 1) * BLK]
-        for place in range(GROUP):
-            turned = got[place * BLK : (place + 1) * BLK].T
-            values[p, :BLK, pl.ds(row_at[place], BLK)] = turned.astype(BF16)
-        values[p, :BLK, CLIP_ROWS:end] = got[CLIP_ROWS:].T.astype(BF16)
-        values[p, BLK:, :end] = jnp.ones((PAD, end), BF16)
+    for j in range(0, width, tile):
+        got = jnp.dot(normed[...], weights[2, :, j : j + tile], preferred_element_type=F32)
+        for k in range(tile // BLK):
+            p = j // BLK + k
+            cols = slice(k * BLK, (k + 1) * BLK)
+            for place in range(last):
+                turned = got[place * BLK : (place + 1) * BLK, cols].T
+                values[p, :BLK, pl.ds(row_at[place], BLK)] = turned.astype(BF16)
     for b in range(2, SLOT_DEV):
 
         @pl.when(b >= length)
         def _():
             values[:, :BLK, b * BLK : (b + 1) * BLK] = jnp.zeros((pairs, BLK, BLK), BF16)
 
+    visit_blocks(info, (1, 2), query, keys, values, context)
+    across[...] = context[0]
+    far[...] = context[1]
+    keep.wait()
+
+
+def rest_kernel(query, keys, values, facts, near, own, context, info, sems):
+    load = pltpu.make_async_copy(facts, info, sems.at[0])
+    load.start()
+    width = query.shape[1]
+    pairs = width // BLK
     context[...] = jnp.zeros_like(context)
-    low = lax.broadcasted_iota(jnp.int32, (BLK, BLK), 1) < HEAD_DIM
-    real = lax.broadcasted_iota(jnp.int32, (PAD, 2 * BLK), 0) < NB
-    nt = (((1,), (1,)), ((), ()))
-
-    def token_block(place, block, first, count):
-        start = pl.multiple_of(first * BLK, BLK)
-        at = pl.multiple_of(block * BLK, BLK)
-        seen = count * BLK
-        cols = [slice(p * BLK, (p + 1) * BLK) for p in range(pairs)]
-        scores = []
-        for p in range(pairs):
-            q = query[pl.ds(at, BLK), cols[p]]
-            none = jnp.zeros_like(q)
-            both = jnp.concatenate([jnp.where(low, q, none), jnp.where(low, none, q)], axis=0)
-            k = jnp.concatenate([keys[pl.ds(start, seen), cols[p]], keys[CLIP_ROWS:end, cols[p]]], axis=0)
-            s = lax.dot_general(k, both, nt, preferred_element_type=F32)
-            scores.append((s[:seen], jnp.where(real, s[seen:], -1e30)))
-        tops = [
-            jnp.maximum(jnp.max(s, axis=0, keepdims=True), jnp.max(se, axis=0, keepdims=True))
-            for s, se in scores
-        ]
-        parts = [
-            jnp.concatenate([jnp.exp(s - top).astype(BF16), jnp.exp(se - top).astype(BF16)], axis=0)
-            for (s, se), top in zip(scores, tops)
-        ]
-        sums = []
-        for p in range(pairs):
-            v = jnp.concatenate([values[p, :, pl.ds(start, seen)], values[p, :, CLIP_ROWS:end]], axis=1)
-            sums.append(jnp.dot(v, parts[p], preferred_element_type=F32))
-        for p in range(pairs):
-            o = sums[p]
-            total = o[BLK : BLK + 1]
-            o = jnp.concatenate(
-                [o[:HEAD_DIM, :BLK] / total[:, :BLK], o[HEAD_DIM:BLK, BLK:] / total[:, BLK:]], axis=0
-            )
-            context[place, :, cols[p]] = o.T.astype(BF16)
-
-    def visit(place, carry):
-        block = info[place]
-        is_video = block < video
-        first = jnp.where(is_video, 0, video)
-        seen = jnp.where(is_video, video, length - video)
-        for count in range(1, SLOT_DEV):
-
-            @pl.when((block >= 0) & (seen == count))
-            def _():
-                token_block(place, block, first, count)
-
-        return carry
-
-    lax.fori_loop(0, GROUP, visit, 0)
+    load.wait()
+    length = info[0, GROUP]
+    video = info[0, GROUP + 1]
+    visit_blocks(info, (0, 3), query, keys, values, context)
+    near[...] = context[0]
+    own[:BLK, :] = context[1]
 
     heads = width // HEAD_DIM
     sub = 8
-    qe = query[CLIP_ROWS:end, :].astype(F32)[:sub]
+    qe = query[CLIP_ROWS:END, :].astype(F32)[:sub]
     qe = jnp.concatenate([qe] * heads, axis=0)
     row_head = lax.broadcasted_iota(jnp.int32, (heads * sub, width), 0) // sub
     col_head = lax.broadcasted_iota(jnp.int32, (heads * sub, width), 1) // HEAD_DIM
     qe = jnp.where(row_head == col_head, qe, 0.0).astype(BF16)
-    s = lax.dot_general(qe, keys[:end, :], nt, preferred_element_type=F32)
+    s = lax.dot_general(qe, keys[:END, :], NT, preferred_element_type=F32)
     col = lax.broadcasted_iota(jnp.int32, s.shape, 1)
     bottle = (col >= CLIP_ROWS) & (col < CLIP_ROWS + NB)
     parts = []
@@ -257,14 +315,10 @@
     for p in range(pairs):
         rows = slice(2 * p * sub, (2 * p + 2) * sub)
         both = jnp.concatenate([parts[0][rows], parts[1][rows]], axis=0)
-        o = lax.dot_general(both, values[p, :BLK, :end], nt, preferred_element_type=F32)
+        o = lax.dot_general(both, values[p, :BLK, :END], NT, preferred_element_type=F32)
         o = 0.5 * (o[: 2 * sub] + o[2 * sub :])
         o = jnp.where(first_head, o[:sub], o[sub:])
         own[BLK:, p * BLK : (p + 1) * BLK] = jnp.concatenate([o, jnp.zeros_like(o)], axis=0).astype(BF16)
-    near[...] = context[0]
-    across[...] = context[1]
-    far[...] = context[2]
-    own[:BLK, :] = context[3]
 
 
 def feed_kernel(
@@ -353,42 +407,92 @@
     return pltpu.with_memory_space_constraint(x, pltpu.HBM)
 
 
-def attend(slots, clip_lengths, video_blocks, stored_all, arrived, gain1, w_qkv):
-    width = stored_all.shape[2]
-    model = 2 * width
-    heads_width = w_qkv.shape[2]
+def ready(slots, gain1, w_qkv, stored_all):
+    model = w_qkv.shape[1]
+    width = w_qkv.shape[2]
+    pairs = width // BLK
+    return pl.pallas_call(
+        ready_kernel,
+        name="ready",
+        out_shape=(
+            spec(w_qkv.shape),
+            spec((BLK + PAD, width)),
+            spec((BLK + PAD, width)),
+            spec((pairs, BLK, BLK + PAD)),
+        ),
+        in_specs=[HBM, HBM, HBM, VMEM],
+        out_specs=(VMEM,) * 4,
+        scratch_shapes=[
+            pltpu.VMEM((BLK + PAD, model), BF16),
+            pltpu.VMEM((1, model), F32),
+            pltpu.SMEM(slots.shape, jnp.int32),
+            DMA((5,)),
+        ],
+        compiler_params=pltpu.CompilerParams(vmem_limit_bytes=8 << 20),
+        cost_estimate=pl.CostEstimate(flops=450000000, bytes_accessed=4000000, transcendentals=0),
+    )(stay(slots), stay(gain1), stay(w_qkv), stored_all)
+
+
+def attend(slots, clip_lengths, video_blocks, gain1, arrived, weights, own_qkv):
+    model = weights.shape[1]
+    width = weights.shape[2]
+    pairs = width // BLK
+    rows = CLIP_ROWS + 2 * BLK
     block = spec((BLK, width))
+    info = (1, 2 * GROUP)
     return pl.pallas_call(
         attend_kernel,
         name="attend",
-        out_shape=(block, block, block, spec((BLK + PAD, width))),
-        in_specs=[HBM, HBM, HBM, VMEM, VMEM, HBM, HBM],
-        out_specs=(VMEM,) * 4,
+        out_shape=(
+            block,
+            block,
+            spec((rows, width)),
+            spec((rows, width)),
+            spec((pairs, BLK + PAD, rows)),
+            spec(info, jnp.int32),
+        ),
+        in_specs=[HBM] * 4 + [VMEM] * 5,
+        out_specs=(VMEM,) * 6,
         scratch_shapes=[
-            pltpu.VMEM((CLIP_ROWS + PAD, model), BF16),
-            pltpu.VMEM((CLIP_ROWS + 2 * BLK, heads_width), BF16),
-            pltpu.VMEM((CLIP_ROWS + 2 * BLK, heads_width), BF16),
-            pltpu.VMEM((heads_width // BLK, BLK + PAD, CLIP_ROWS + 2 * BLK), BF16),
-            pltpu.VMEM((GROUP, BLK, heads_width), BF16),
-            pltpu.VMEM(w_qkv.shape, BF16),
-            pltpu.SMEM((GROUP,), jnp.int32),
+            pltpu.VMEM(((GROUP - 1) * BLK, model), BF16),
+            pltpu.VMEM((2, BLK, width), BF16),
+            pltpu.SMEM(info, jnp.int32),
             pltpu.VMEM((1, model), F32),
             pltpu.SMEM(slots.shape, jnp.int32),
             pltpu.SMEM(clip_lengths.shape, jnp.int32),
             pltpu.SMEM(video_blocks.shape, jnp.int32),
-            DMA((7,)),
+            DMA((5,)),
         ],
-        compiler_params=pltpu.CompilerParams(vmem_limit_bytes=24 << 20),
-        cost_estimate=pl.CostEstimate(flops=2500000000, bytes_accessed=6000000, transcendentals=3000000),
+        compiler_params=pltpu.CompilerParams(vmem_limit_bytes=16 << 20),
+        cost_estimate=pl.CostEstimate(flops=1800000000, bytes_accessed=6000000, transcendentals=1500000),
     )(
         stay(slots),
         stay(clip_lengths),
         stay(video_blocks),
-        stored_all,
+        stay(gain1),
         arrived,
-        stay(gain1),
-        stay(w_qkv),
+        weights,
+        *own_qkv,
     )
+
+
+def rest(query, keys, values, facts):
+    width = query.shape[1]
+    info = (1, 2 * GROUP)
+    return pl.pallas_call(
+        rest_kernel,
+        name="rest",
+        out_shape=(spec((BLK, width)), spec((BLK + PAD, width))),
+        in_specs=[VMEM] * 4,
+        out_specs=(VMEM,) * 2,
+        scratch_shapes=[
+            pltpu.VMEM((2, BLK, width), BF16),
+            pltpu.SMEM(info, jnp.int32),
+            DMA((1,)),
+        ],
+        compiler_params=pltpu.CompilerParams(vmem_limit_bytes=16 << 20),
+        cost_estimate=pl.CostEstimate(flops=700000000, bytes_accessed=3000000, transcendentals=1500000),
+    )(query, keys, values, facts)
 
 
 def feed(slots, stored_all, own_all, arrived, w_out, w_out_other, gain2, w_up, w_down):
@@ -451,14 +555,17 @@
     near = partner(near, 1)
     far = partner(far, 2)
     stored_all = lax.all_gather(stored, "mp", axis=0)
+    weights, *own_qkv = ready(slots, gain1, w_qkv, stored_all)
     arrived = lax.all_gather(jnp.concatenate([near, across, far], axis=0), "mp", axis=0)
 
-    near, across, far, own = attend(
-        slots, clip_lengths, video_blocks, stored_all, arrived, gain1, w_qkv
+    across, far, query, keys, values, facts = attend(
+        slots, clip_lengths, video_blocks, gain1, arrived, weights, own_qkv
     )
+    far = partner(far, 2)
     across = partner(across, 3)
+    near, own = rest(query, keys, values, facts)
     near = partner(near, 1)
-    far = partner(far, 2)
+    own, far, across = lax.optimization_barrier((own, far, across))
     own_all = lax.all_gather(own, "mp", axis=0)
     arrived = lax.all_gather(jnp.concatenate([near, across, far], axis=0), "mp", axis=0)
 

time: 47.5 us -> 45.9 us (0.966); the launches traced: 47.9 us -> 45.7 us
  blocking collectives: 15 us -> 12.1 us
    all_gather x2, blocking collectives: 6.91 us -> 4.74 us  [body(): lax.all_gather(jnp.concatenate([near, across, far], axis=0), 'mp', axis=0)]
    all_gather x1, blocking collectives: 2.86 us -> 2.13 us  [body(): own_all = lax.all_gather(own, 'mp', axis=0)]
    pallas_call x1 -> x3, Pallas kernels: 8.33 us -> 8.19 us  [the longest x1 3.75 us: attend(): pl.pallas_call(attend_kernel, name='attend', out_shape=(block, block, spe...]
  transfers between devices with their start and end apart: 7 -> 7, of which waited for: 1 -> 2; matrix products, arithmetic and copies ran while one was open for 0% -> 0% of each run, Pallas kernels for 17% -> 18%
where the time goes in v3:
time: 45.9 us; the launch traced here: 45.7 us
  Pallas kernels  17.5 us (38%)
  blocking collectives  12.1 us (26%)
  starting transfers between devices  11.2 us (24%)
  waiting for transfers between devices  3.98 us (9%)
  between operations  0.77 us (2%)
    ppermute x6, starting transfers between devices, partner(): lax.ppermute(x, 'clip', [(i, i ^ step) for i in range(lax.axis_size('clip...  8.39 us
    pallas_call x1, Pallas kernels, feed(): pl.pallas_call(feed_kernel, name='feed', out_shape=(spec((ROWS, width), F...  5.91 us
    all_gather x2, blocking collectives, body(): lax.all_gather(jnp.concatenate([near, across, far], axis=0), 'mp', axis=0)  4.74 us
    ppermute x6, waiting for transfers between devices, partner(): lax.ppermute(x, 'clip', [(i, i ^ step) for i in range(lax.axis_size('clip...  3.98 us
    pallas_call x1, Pallas kernels, attend(): pl.pallas_call(attend_kernel, name='attend', out_shape=(block, block, spe...  3.75 us
    all_gather x1, blocking collectives, body(): stored_all = lax.all_gather(stored, 'mp', axis=0)  2.87 us
    ppermute x1, starting transfers between devices, body(): w_out_other = lax.ppermute(w_out, 'mp', [(0, 1), (1, 0)])  2.84 us
    pallas_call x1, Pallas kernels, ready(): pl.pallas_call(ready_kernel, name='ready', out_shape=(spec(w_qkv.shape),...  2.41 us
  transfers between devices with their start and end apart: 7, of which 2 were waited for; matrix products, arithmetic and copies ran while one was open for 0% of the time, Pallas kernels for 18%

profile of v3, /device:TPU:1, one launch (start us, length us, event | category | flops | bytes accessed | tf_op | source)
XLA Modules:
  0.0 45.7 jit_solution(7969260106015918864)
XLA Ops:
  0.6 2.0 %pack.1 = (bf16[128,512]{1,0:T(8,128)(2,1)S(1)}, bf16[128,512]{1,0:T(8,128)(2,1)S(1)}, bf16[128,512]{1,0:T(8,128)(2,1)S(1)}, bf16[400,512]{1,0:T(8,128)(2,1)S(1)}) custom-call(s32[3,128]{1,0:T(4,128)} %bitcast.14, bf16[3,128,512]{2,1,0:T(8,128)(2,1)} %tokens.1, bf16[1,4,512]{2,1,0:T(4,128)(2,1)} %extra.1), custom_call_target="tpu_custom_call" | custom-call | tf_op jit(solution)/shard_map/pack/pallas_call | solution.py:540
  2.6 2.1 %collective-permute-start = (bf16[128,512]{1,0:T(8,128)(2,1)S(1)}, bf16[128,512]{1,0:T(8,128)(2,1)S(1)}, u32[]{:S(2)}, u32[]{:S(2)}) collective-permute-start(bf16[128,512]{1,0:T(8,128)(2,1)S(1)} %get-tuple-element.24), channel_id=1, source_target_pairs={{0,2},{2,0},{4,6},{6,4},{8,10},{10,8},{12,14},{14,12},{16,18},{18,... | collective-permute-start | bytes 393224 | tf_op jit(solution)/shard_map/ppermute | solution.py:32
  4.7 1.8 %collective-permute-start.1 = (bf16[128,512]{1,0:T(8,128)(2,1)S(1)}, bf16[128,512]{1,0:T(8,128)(2,1)S(1)}, u32[]{:S(2)}, u32[]{:S(2)}) collective-permute-start(bf16[128,512]{1,0:T(8,128)(2,1)S(1)} %get-tuple-element.25), channel_id=1, source_target_pairs={{0,6},{2,4},{4,2},{6,0},{8,14},{10,12},{12,10},{14,8},{16,22},{18,... | collective-permute-start | bytes 393224 | tf_op jit(solution)/shard_map/ppermute | solution.py:32
  6.6 0.6 %collective-permute-start.2 = (bf16[128,512]{1,0:T(8,128)(2,1)S(1)}, bf16[128,512]{1,0:T(8,128)(2,1)S(1)}, u32[]{:S(2)}, u32[]{:S(2)}) collective-permute-start(bf16[128,512]{1,0:T(8,128)(2,1)S(1)} %get-tuple-element.26), channel_id=1, source_target_pairs={{0,4},{2,6},{4,0},{6,2},{8,12},{10,14},{12,8},{14,10},{16,20},{18,... | collective-permute-start | bytes 393224 | tf_op jit(solution)/shard_map/ppermute | solution.py:32
  7.2 2.8 %collective-permute-start.6 = (bf16[512,1024]{1,0:T(8,128)(2,1)}, bf16[512,1024]{1,0:T(8,128)(2,1)S(1)}, u32[]{:S(2)}, u32[]{:S(2)}) collective-permute-start(bf16[512,1024]{1,0:T(8,128)(2,1)} %w_out.1), channel_id=1, source_target_pairs={{0,1},{1,0},{2,3},{3,2},{4,5},{5,4},{6,7},{7,6},{8,9},{9,8},{10,11... | collective-permute-start | bytes 3145736 | tf_op jit(solution)/shard_map/ppermute | solution.py:537
  10.0 2.9 %all-gather = bf16[800,512]{1,0:T(8,128)(2,1)S(1)} all-gather(bf16[400,512]{1,0:T(8,128)(2,1)S(1)} %get-tuple-element.23), channel_id=2, replica_groups=mesh['clip'=128,'mp'=2] {'mp'}, dimensions={0}, use_global_device_ids=true | all-gather | bytes 1228800 | tf_op jit(solution)/shard_map/all_gather | solution.py:557
  12.9 2.4 %ready.1 = (bf16[3,1024,512]{2,1,0:T(8,128)(2,1)S(1)}, bf16[144,512]{1,0:T(8,128)(2,1)S(1)}, bf16[144,512]{1,0:T(8,128)(2,1)S(1)}, bf16[4,128,144]{2,1,0:T(8,128)(2,1)S(1)}) custom-call(s32[3,128]{1,0:T(4,128)} %bitcast.15, f32[1,1024]{1,0:T(1,128)} %bitcast.20, bf16[3,1024,512]{2,1,0:T(8,128)(2,1)} %w_qkv.1, bf16[2,400,512]{2,1,0:T(8,128)(2,1)S(1)} %bitcast.8), custom_call_target="tpu_custom_call" | custom-call | flops 450000000 | bytes 4000000 | tf_op jit(solution)/shard_map/ready/pallas_call | solution.py:414
  15.3 0.0 collective-permute-done
  15.3 0.0 collective-permute-done.1
  15.4 0.0 collective-permute-done.2
  15.4 2.4 %all-gather.1 = bf16[768,512]{1,0:T(8,128)(2,1)S(1)} all-gather(bf16[384,512]{1,0:T(8,128)(2,1)S(1)} %pad_maximum_fusion), channel_id=3, replica_groups=mesh['clip'=128,'mp'=2] {'mp'}, dimensions={0}, use_global_device_ids=true | all-gather | bytes 1179648 | tf_op jit(solution)/shard_map/all_gather | solution.py:559
  17.8 0.0 copy-start.2
  17.8 3.7 %attend.1 = (bf16[128,512]{1,0:T(8,128)(2,1)S(1)}, bf16[128,512]{1,0:T(8,128)(2,1)S(1)}, bf16[768,512]{1,0:T(8,128)(2,1)S(1)}, bf16[768,512]{1,0:T(8,128)(2,1)S(...) custom-call(s32[3,128]{1,0:T(4,128)} %bitcast.16, s32[128]{0:T(128)} %all_lengths.1, s32[128]{0:T(128)} %all_videos.1, ...), custom_call_target="tpu_custom_call" | custom-call | flops 1800000000 | bytes 6000000 | tf_op jit(solution)/shard_map/attend/pallas_call | solution.py:443
  21.5 0.0 copy-start
  21.5 0.0 copy-start.1
  21.5 0.0 copy-start.3
  21.6 0.0 copy-start.4
  21.6 2.0 %collective-permute-start.3 = (bf16[128,512]{1,0:T(8,128)(2,1)S(1)}, bf16[128,512]{1,0:T(8,128)(2,1)S(1)}, u32[]{:S(2)}, u32[]{:S(2)}) collective-permute-start(bf16[128,512]{1,0:T(8,128)(2,1)S(1)} %get-tuple-element.36), channel_id=1, source_target_pairs={{0,4},{2,6},{4,0},{6,2},{8,12},{10,14},{12,8},{14,10},{16,20},{18,... | collective-permute-start | bytes 393224 | tf_op jit(solution)/shard_map/ppermute | solution.py:32
  23.6 0.2 collective-permute-start.4
  23.9 2.0 %rest.1 = (bf16[128,512]{1,0:T(8,128)(2,1)S(1)}, bf16[144,512]{1,0:T(8,128)(2,1)S(1)}) custom-call(bf16[768,512]{1,0:T(8,128)(2,1)S(1)} %get-tuple-element.31.query, bf16[768,512]{1,0:T(8,128)(2,1)S(1)} %get-tuple-element.32.keys, bf16[4,144,768]{2,1,0:T(8,128)(2,1)S(1)} %get-tuple-element.33.values, s32[1,8]{1,0:T(1,128)S(1)} %get-tuple-element.34.facts), custom_call_target="tpu_custom_call" | custom-call | flops 700000000 | bytes 3000000 | tf_op jit(solution)/shard_map/rest/pallas_call | solution.py:482
  25.9 1.5 %collective-permute-start.5 = (bf16[128,512]{1,0:T(8,128)(2,1)S(1)}, bf16[128,512]{1,0:T(8,128)(2,1)S(1)}, u32[]{:S(2)}, u32[]{:S(2)}) collective-permute-start(bf16[128,512]{1,0:T(8,128)(2,1)S(1)} %get-tuple-element.39), channel_id=1, source_target_pairs={{0,2},{2,0},{4,6},{6,4},{8,10},{10,8},{12,14},{14,12},{16,18},{18,... | collective-permute-start | bytes 393224 | tf_op jit(solution)/shard_map/ppermute | solution.py:32
  27.4 0.5 collective-permute-done.3
  27.9 3.5 %collective-permute-done.4 = bf16[128,512]{1,0:T(8,128)(2,1)S(1)} collective-permute-done((bf16[128,512]{1,0:T(8,128)(2,1)S(1)}, bf16[128,512]{1,0:T(8,128)(2,1)S(1)}, u32[]{:S(2)}, u32[]{:S(2)}) %collective-permute-start.4) | collective-permute-done | bytes 131104 | tf_op jit(solution)/shard_map/ppermute | solution.py:32
  31.4 2.1 %all-gather.2 = bf16[288,512]{1,0:T(8,128)(2,1)S(1)} all-gather(bf16[144,512]{1,0:T(8,128)(2,1)S(1)} %get-tuple-element.38), channel_id=4, replica_groups=mesh['clip'=128,'mp'=2] {'mp'}, dimensions={0}, use_global_device_ids=true | all-gather | bytes 442368 | tf_op jit(solution)/shard_map/all_gather | solution.py:569
  33.5 0.0 collective-permute-done.5
  33.6 2.4 %all-gather.3 = bf16[768,512]{1,0:T(8,128)(2,1)S(1)} all-gather(bf16[384,512]{1,0:T(8,128)(2,1)S(1)} %pad_maximum_fusion.1), channel_id=5, replica_groups=mesh['clip'=128,'mp'=2] {'mp'}, dimensions={0}, use_global_device_ids=true | all-gather | bytes 1179648 | tf_op jit(solution)/shard_map/all_gather | solution.py:570
  35.9 0.0 collective-permute-done.6.w_out_other
  35.9 0.0 copy-done.2
  35.9 0.0 copy-done
  35.9 0.0 copy-done.1
  36.0 0.0 copy-done.3
  36.0 0.0 copy-done.4
  36.0 5.9 %feed.1 = (f32[400,512]{1,0:T(8,128)S(1)}, bf16[400,512]{1,0:T(8,128)(2,1)S(1)}) custom-call(s32[3,128]{1,0:T(4,128)S(1)} %bitcast.17, bf16[2,400,512]{2,1,0:T(8,128)(2,1)S(1)} %bitcast.9, bf16[2,144,512]{2,1,0:T(8,128)(2,1)S(1)} %bitcast.13, bf16[2,384,512]{2,1,0:T(8,128)(2,1)S(1)} %bitcast.12, bf16[512,1024]{1,0:T(8,128)(2,1)S(1)} %copy-done.3, ...), custom_call_target="tpu_custom_call" | custom-call | flops 4100000000 | bytes 14000000 | tf_op jit(solution)/shard_map/feed/pallas_call | solution.py:502
  41.9 2.4 %all-gather.4 = bf16[800,512]{1,0:T(8,128)(2,1)S(1)} all-gather(bf16[400,512]{1,0:T(8,128)(2,1)S(1)} %get-tuple-element.43), channel_id=6, replica_groups=mesh['clip'=128,'mp'=2] {'mp'}, dimensions={0}, use_global_device_ids=true | all-gather | bytes 1228800 | tf_op jit(solution)/shard_map/all_gather | solution.py:575
  44.3 1.4 %finish.1 = (bf16[3,128,512]{2,1,0:T(8,128)(2,1)}, bf16[1,4,512]{2,1,0:T(4,128)(2,1)}) custom-call(s32[3,128]{1,0:T(4,128)S(1)} %bitcast.18, f32[400,512]{1,0:T(8,128)S(1)} %get-tuple-element.42.base, bf16[2,400,512]{2,1,0:T(8,128)(2,1)S(1)} %bitcast.10), custom_call_target="tpu_custom_call" | custom-call | tf_op jit(solution)/shard_map/finish/pallas_call | solution.py:577
  (2 shorter events, 0.1 us)
Async XLA Ops:
  2.6 12.7 %collective-permute-start = (bf16[128,512]{1,0:T(8,128)(2,1)S(1)}, bf16[128,512]{1,0:T(8,128)(2,1)S(1)}, u32[]{:S(2)}, u32[]{:S(2)}) collective-permute-start(bf16[128,512]{1,0:T(8,128)(2,1)S(1)} %get-tuple-element.24), channel_id=1, source_target_pairs={{0,2},{2,0},{4,6},{6,4},{8,10},{10,8},{12,14},{14,12},{16,18},{18,... | collective-permute-start | bytes 393224 | tf_op jit(solution)/shard_map/ppermute | solution.py:32
  4.7 10.6 %collective-permute-start.1 = (bf16[128,512]{1,0:T(8,128)(2,1)S(1)}, bf16[128,512]{1,0:T(8,128)(2,1)S(1)}, u32[]{:S(2)}, u32[]{:S(2)}) collective-permute-start(bf16[128,512]{1,0:T(8,128)(2,1)S(1)} %get-tuple-element.25), channel_id=1, source_target_pairs={{0,6},{2,4},{4,2},{6,0},{8,14},{10,12},{12,10},{14,8},{16,22},{18,... | collective-permute-start | bytes 393224 | tf_op jit(solution)/shard_map/ppermute | solution.py:32
  6.6 8.8 %collective-permute-start.2 = (bf16[128,512]{1,0:T(8,128)(2,1)S(1)}, bf16[128,512]{1,0:T(8,128)(2,1)S(1)}, u32[]{:S(2)}, u32[]{:S(2)}) collective-permute-start(bf16[128,512]{1,0:T(8,128)(2,1)S(1)} %get-tuple-element.26), channel_id=1, source_target_pairs={{0,4},{2,6},{4,0},{6,2},{8,12},{10,14},{12,8},{14,10},{16,20},{18,... | collective-permute-start | bytes 393224 | tf_op jit(solution)/shard_map/ppermute | solution.py:32
  7.2 28.7 %collective-permute-start.6 = (bf16[512,1024]{1,0:T(8,128)(2,1)}, bf16[512,1024]{1,0:T(8,128)(2,1)S(1)}, u32[]{:S(2)}, u32[]{:S(2)}) collective-permute-start(bf16[512,1024]{1,0:T(8,128)(2,1)} %w_out.1), channel_id=1, source_target_pairs={{0,1},{1,0},{2,3},{3,2},{4,5},{5,4},{6,7},{7,6},{8,9},{9,8},{10,11... | collective-permute-start | bytes 3145736 | tf_op jit(solution)/shard_map/ppermute | solution.py:537
  17.8 18.2 %copy-start.2 = (bf16[2048,1024]{1,0:T(8,128)(2,1)S(1)}, bf16[2048,1024]{1,0:T(8,128)(2,1)}, u32[]{:S(2)}) copy-start(bf16[2048,1024]{1,0:T(8,128)(2,1)} %w_down.1) | copy-start | bytes 12582916
  21.5 14.4 %copy-start = (s32[128,3]{0,1:T(4,128)S(1)}, s32[128,3]{0,1:T(4,128)}, u32[]{:S(2)}) copy-start(s32[128,3]{0,1:T(4,128)} %param.15) | copy-start | bytes 4612
  21.5 14.4 %copy-start.1 = (bf16[1024,2048]{1,0:T(8,128)(2,1)S(1)}, bf16[1024,2048]{1,0:T(8,128)(2,1)}, u32[]{:S(2)}) copy-start(bf16[1024,2048]{1,0:T(8,128)(2,1)} %w_up.1) | copy-start | bytes 12582916
  21.5 14.4 %copy-start.3 = (bf16[512,1024]{1,0:T(8,128)(2,1)S(1)}, bf16[512,1024]{1,0:T(8,128)(2,1)}, u32[]{:S(2)}) copy-start(bf16[512,1024]{1,0:T(8,128)(2,1)} %w_out.1) | copy-start | bytes 3145732
  21.6 14.4 %copy-start.4 = (f32[1024]{0:T(1024)S(1)}, f32[1024]{0:T(1024)}, u32[]{:S(2)}) copy-start(f32[1024]{0:T(1024)} %param.19) | copy-start | bytes 12292
  21.6 6.3 %collective-permute-start.3 = (bf16[128,512]{1,0:T(8,128)(2,1)S(1)}, bf16[128,512]{1,0:T(8,128)(2,1)S(1)}, u32[]{:S(2)}, u32[]{:S(2)}) collective-permute-start(bf16[128,512]{1,0:T(8,128)(2,1)S(1)} %get-tuple-element.36), channel_id=1, source_target_pairs={{0,4},{2,6},{4,0},{6,2},{8,12},{10,14},{12,8},{14,10},{16,20},{18,... | collective-permute-start | bytes 393224 | tf_op jit(solution)/shard_map/ppermute | solution.py:32
  23.6 7.8 %collective-permute-start.4 = (bf16[128,512]{1,0:T(8,128)(2,1)S(1)}, bf16[128,512]{1,0:T(8,128)(2,1)S(1)}, u32[]{:S(2)}, u32[]{:S(2)}) collective-permute-start(bf16[128,512]{1,0:T(8,128)(2,1)S(1)} %get-tuple-element.37), channel_id=1, source_target_pairs={{0,6},{2,4},{4,2},{6,0},{8,14},{10,12},{12,10},{14,8},{16,22},{18,... | collective-permute-start | bytes 393224 | tf_op jit(solution)/shard_map/ppermute | solution.py:32
  25.9 7.6 %collective-permute-start.5 = (bf16[128,512]{1,0:T(8,128)(2,1)S(1)}, bf16[128,512]{1,0:T(8,128)(2,1)S(1)}, u32[]{:S(2)}, u32[]{:S(2)}) collective-permute-start(bf16[128,512]{1,0:T(8,128)(2,1)S(1)} %get-tuple-element.39), channel_id=1, source_target_pairs={{0,2},{2,0},{4,6},{6,4},{8,10},{10,8},{12,14},{14,12},{16,18},{18,... | collective-permute-start | bytes 393224 | tf_op jit(solution)/shard_map/ppermute | solution.py:32
